TPU v7x, 32 devices: a whole 2x2x4 slice. The times are simulated.
32 devices in a mesh: groups: 2 (over x), queue: 16 (over z, y, core).
Axes of the slice: x: 2, y: 2, z: 4, core: 2. Of those that a mesh axis runs over, the one named last changes fastest.
Arguments:
- hidden: bfloat16 [256, 5120], P(('groups', 'queue')), parts along dimension 0, may hold values from -6 to 6
- incoming: bfloat16 [2, 16, 5120], P(None, 'groups'), parts along dimension 1, may hold values from -6 to 6
- levels: int32 [16], replicated, may hold values from 0 to 95, as said below
- mod_table: bfloat16 [96, 3, 5120], replicated, may hold values from -3 to 3
- query_weight: bfloat16 [5120, 5120], P(None, 'queue'), may hold values from -0.078125 to 0.078125
- key_weight: bfloat16 [5120, 5120], P(None, 'queue'), may hold values from -0.078125 to 0.078125
- value_weight: bfloat16 [5120, 5120], P(None, 'queue'), may hold values from -0.078125 to 0.078125
- output_weight: bfloat16 [5120, 5120], P(None, 'queue'), may hold values from -0.078125 to 0.078125
- query_gain: float32 [5120], replicated, may hold values from 0.5 to 1.5
- key_gain: float32 [5120], replicated, may hold values from 0.5 to 1.5
- text_keys: bfloat16 [1024, 5120], P(('groups', 'queue')), parts along dimension 0, may hold values from -6 to 6
- text_values: bfloat16 [1024, 5120], P(('groups', 'queue')), parts along dimension 0, may hold values from -6 to 6
Outputs:
- updated: bfloat16 [256, 5120], P(('groups', 'queue')), parts along dimension 0
There are 2 independent parts, one for each index of `groups`. A program takes and returns all parts, laid end to end along the dimension named above; an argument that names none is the same for every part. Nothing has to cross between parts.
Inputs may be any that keep to these rules, and one draw needn't show every extreme that they name: `levels`: strictly rising along the queue positions; the last position always has level 95.
All inputs are finite; a program needn't handle non-finite values.
Results may differ from a plain program's by a relative error of at most 0.0085.
Values may be sent and summed in bfloat16 or wider, within the bound.
A program may use at most 128 MiB of HBM per device.

v0:
```python
import functools
import math

import jax
import jax.numpy as jnp
from jax import lax
from jax.experimental import pallas as pl
from jax.experimental.pallas import tpu as pltpu
from jax.sharding import PartitionSpec as P

HEADS = 40
STEPS = 2
FIRST_CHUNKS = 2
CHUNKS = 2


def passed_along(value, axis, steps):
    count = lax.axis_size(axis)
    initial, last = (max(0, -steps), min(count, count - steps))
    return lax.ppermute(value, axis, [(source, source + steps) for source in range(initial, last)])


def normalize(values):
    return values * lax.rsqrt(jnp.mean(values * values, axis=-1, keepdims=True) + 1e-06)


def softmax_rounded(scores):
    row_max = jnp.max(scores, axis=-1, keepdims=True)
    weights = jnp.exp(scores - row_max)
    return (weights / jnp.sum(weights, axis=-1, keepdims=True)).astype(jnp.bfloat16)


def pad_slots(values, slot_total):
    missing = slot_total - values.shape[1]
    filler = jnp.zeros((values.shape[0], missing, values.shape[2]), values.dtype)
    return jnp.concatenate([values, filler], axis=1)


def causal_block(queries, keys_all, values_all, span_rows, score_scale):
    total_rows = queries.shape[0]
    block_rows = min(512, total_rows)
    scores = (
        jnp.einsum("qsd,ksd->sqk", queries, keys_all, preferred_element_type=jnp.float32)
        * score_scale
    )
    allowed = (
        jnp.arange(0, block_rows)[:, None] // span_rows
        >= jnp.arange(block_rows)[None, :] // span_rows
    )
    scores = jnp.where(allowed[None], scores, -1e30)
    result = jnp.einsum(
        "sqk,ksd->qsd", softmax_rounded(scores), values_all, preferred_element_type=jnp.float32
    )
    pieces = result.astype(jnp.bfloat16)
    return pieces


def text_attend(queries, text_k, text_v, score_scale):
    scores = (
        jnp.einsum("qsd,tsd->sqt", queries, text_k, preferred_element_type=jnp.float32)
        * score_scale
    )
    return jnp.einsum(
        "sqt,tsd->qsd", softmax_rounded(scores), text_v, preferred_element_type=jnp.float32
    ).astype(jnp.bfloat16)


def per_device(
    hidden,
    incoming,
    levels,
    mod_table,
    query_weight,
    key_weight,
    value_weight,
    output_weight,
    query_gain,
    key_gain,
    text_keys,
    text_values,
):
    own_index = lax.axis_index("queue")
    queue_size = lax.axis_size("queue")
    span_rows, model_width = hidden.shape
    head_size = model_width // HEADS
    score_scale = 1.0 / math.sqrt(head_size)
    slot_total = -(-HEADS // queue_size) * queue_size
    own_level = lax.dynamic_index_in_dim(levels, own_index, 0, keepdims=False)
    modulation = lax.dynamic_index_in_dim(mod_table, own_level, 0, keepdims=False).astype(
        jnp.float32
    )
    stacked_weights = jnp.stack([query_weight, key_weight, value_weight])
    text_local = text_keys.shape[0]
    text_k_slots, text_v_slots = (
        lax.all_to_all(
            pad_slots(text_keys.reshape(text_local, HEADS, head_size), slot_total),
            "queue",
            split_axis=1,
            concat_axis=0,
            tiled=True,
        ),
        lax.all_to_all(
            pad_slots(text_values.reshape(text_local, HEADS, head_size), slot_total),
            "queue",
            split_axis=1,
            concat_axis=0,
            tiled=True,
        ),
    )
    queue_state = hidden
    for section_index in range(STEPS):
        shifted = passed_along(queue_state, "queue", 1)
        queue_state = jnp.where(own_index == 0, incoming[section_index], shifted)
        current = queue_state.astype(jnp.float32)
        modulated = (normalize(current) * (1.0 + modulation[1]) + modulation[0]).astype(
            jnp.bfloat16
        )
        columns = jnp.einsum(
            "rd,cdw->crw",
            lax.all_gather(modulated, "queue", axis=0, tiled=True),
            stacked_weights,
            preferred_element_type=jnp.float32,
        )
        own_rows = lax.all_to_all(
            columns.astype(jnp.bfloat16), "queue", split_axis=1, concat_axis=2, tiled=True
        ).astype(columns.dtype)
        query_heads = (
            (normalize(own_rows[0]) * query_gain)
            .astype(jnp.bfloat16)
            .reshape(span_rows, HEADS, head_size)
        )
        key_heads = (
            (normalize(own_rows[1]) * key_gain)
            .astype(jnp.bfloat16)
            .reshape(span_rows, HEADS, head_size)
        )
        value_heads = own_rows[2].astype(jnp.bfloat16).reshape(span_rows, HEADS, head_size)
        query_slots, key_slots, value_slots = (
            lax.all_to_all(
                pad_slots(query_heads, slot_total), "queue", split_axis=1, concat_axis=0, tiled=True
            ),
            lax.all_to_all(
                pad_slots(key_heads, slot_total), "queue", split_axis=1, concat_axis=0, tiled=True
            ),
            lax.all_to_all(
                pad_slots(value_heads, slot_total), "queue", split_axis=1, concat_axis=0, tiled=True
            ),
        )
        attended_slots = causal_block(query_slots, key_slots, value_slots, span_rows, score_scale)
        crossed_slots = text_attend(query_slots, text_k_slots, text_v_slots, score_scale)
        attended_back, crossed_back = (
            lax.all_to_all(attended_slots, "queue", split_axis=0, concat_axis=1, tiled=True),
            lax.all_to_all(crossed_slots, "queue", split_axis=0, concat_axis=1, tiled=True),
        )
        attended = attended_back[:, :HEADS]
        crossed = crossed_back[:, :HEADS]
        combined = (
            (attended.astype(jnp.float32) + crossed.astype(jnp.float32))
            .astype(jnp.bfloat16)
            .reshape(span_rows, model_width)
        )
        out_columns = jnp.dot(
            lax.all_gather(combined, "queue", axis=0, tiled=True),
            output_weight,
            preferred_element_type=jnp.float32,
        )
        projected = lax.all_to_all(
            out_columns.astype(jnp.bfloat16), "queue", split_axis=0, concat_axis=1, tiled=True
        ).astype(out_columns.dtype)
        queue_state = (current + modulation[2] * projected).astype(jnp.bfloat16)
    return queue_state


def dot_nt(a, b):
    return lax.dot_general(a, b, (((1,), (1,)), ((), ())), preferred_element_type=jnp.float32)


def fused_kernel(
    n,
    cols,
    hidden,
    incoming,
    levels,
    table_hbm,
    wq_hbm,
    wk_hbm,
    wv_hbm,
    wo_hbm,
    q_gain,
    k_gain,
    tkeys,
    tvals,
    out,
    table,
    mods,
    wq,
    wk,
    wv,
    wo,
    first,
    gathered,
    current,
    full,
    placed,
    qb,
    kb,
    vb,
    xsend,
    xrecv,
    ssend,
    srecv,
    tk,
    tv,
    osend,
    orecv,
    load_sems,
    gsend_sems,
    grecv_sems,
    ssend_sems,
    srecv_sems,
    xsend_sems,
    xrecv_sems,
    tsend_sems,
    trecv_sems,
    osend_sems,
    orecv_sems,
):
    me = lax.axis_index("queue")
    span, width = hidden.shape
    head = width // HEADS
    rows = n * span
    pair = 2 * cols
    local = placed.shape[1]
    blocks = gathered.shape[2]
    shared = 2 * local - pair
    step_off = pair - local
    core = lax.rem(me, 2)
    sibling = me + 1 - 2 * core
    across = me + 2 - 4 * lax.rem(me // 2, 2)
    outer = n // 4
    start_col = pl.multiple_of((me // 2) * pair + core * step_off, 128)
    mid = pl.multiple_of((1 - core) * step_off, 128)
    trows = tkeys.shape[0]
    scale = 1.0 / math.sqrt(head)

    loads = [
        pltpu.make_async_copy(s, d, load_sems.at[i])
        for i, (s, d) in enumerate(((wq_hbm, wq), (wk_hbm, wk), (wv_hbm, wv), (wo_hbm, wo)))
    ]
    own = pltpu.make_async_copy(hidden, first.at[me], load_sems.at[4])
    own.start()
    own_table = pltpu.make_async_copy(table_hbm, table, load_sems.at[7])
    own_table.start()
    own_tk = pltpu.make_async_copy(
        tkeys.at[:, pl.ds(start_col, local)], tk.at[pl.ds(me * trows, trows)], load_sems.at[5]
    )
    own_tv = pltpu.make_async_copy(
        tvals.at[:, pl.ds(start_col, local)], tv.at[pl.ds(me * trows, trows)], load_sems.at[6]
    )
    for item in loads + [own_tk, own_tv]:
        item.start()

    own.wait()
    barrier = pltpu.get_barrier_semaphore()
    for k in range(1, n):
        pl.semaphore_signal(
            barrier,
            inc=1,
            device_id={"queue": lax.rem(me + k, n)},
            device_id_type=pl.DeviceIdType.MESH,
        )
    pl.semaphore_wait(barrier, n - 1)

    pending = []

    def remote(src, dst, send, recv, target):
        return pltpu.make_async_remote_copy(
            src_ref=src,
            dst_ref=dst,
            send_sem=send,
            recv_sem=recv,
            device_id={"queue": target},
            device_id_type=pl.DeviceIdType.MESH,
        )

    def gather(view, chunks, phase, between=None):
        bank = phase % 2
        plane = lax.rem(me, 4)
        depth = me // 4

        def copy(slot, ch, kind, target):
            return remote(
                view(slot, ch),
                view(slot, ch),
                gsend_sems.at[bank, kind, slot, ch],
                grecv_sems.at[phase, slot, ch],
                target,
            )

        def push(slot, ch, kind, target):
            copy(slot, ch, kind, target).start()

        def arrived(slot, ch):
            copy(slot, ch, 3, sibling).wait_recv()

        def upward(slot, ch, act):
            @pl.when(depth < outer - 1)
            def _():
                act(copy(slot, ch, 0, lax.rem(me + 4, n)))

        def downward(slot, ch, act):
            @pl.when(depth > 0)
            def _():
                act(copy(slot, ch, 1, lax.rem(me + n - 4, n)))

        def start(c):
            c.start()

        for ch in range(chunks):
            upward(me, ch, start)
            downward(me, ch, start)
            push(me, ch, 2, across)
            push(me, ch, 3, sibling)

        def line(act_in, act_up, act_down, act_side, after=None):
            for d in range(1, outer):
                for ch in range(chunks):

                    @pl.when(depth >= d)
                    def _():
                        slot = lax.rem(me + n - 4 * d, n)
                        act_in(slot, ch)
                        upward(slot, ch, act_up)
                        act_side(slot, ch)

                    @pl.when(depth < outer - d)
                    def _():
                        slot = lax.rem(me + 4 * d, n)
                        act_in(slot, ch)
                        downward(slot, ch, act_down)
                        act_side(slot, ch)
                if after is not None:
                    after(d - 1)

        def sides(slot, ch):
            push(slot, ch, 2, across)
            push(slot, ch, 3, sibling)

        far = [0] + list(range(1, outer))

        def relay(slot, ch):
            arrived(slot, ch)
            push(slot, ch, 3, sibling)

        def other_row(d):
            if d == outer - 2 and between is not None:
                between()
            for ch in range(chunks):
                if d == 0:
                    relay(across, ch)
                else:

                    @pl.when(depth >= d)
                    def _():
                        relay(lax.rem(across + n - 4 * d, n), ch)

                    @pl.when(depth < outer - d)
                    def _():
                        relay(lax.rem(across + 4 * d, n), ch)

        line(arrived, start, start, sides, other_row)
        other_row(outer - 1)
        opposite = me + 3 - 2 * plane
        for base in (sibling, opposite):
            for d in far:
                for ch in range(chunks):
                    arrived(lax.rem(base + n - 4 * d, n), ch)

        def sent(c):
            c.wait_send()

        def finish():
            for ch in range(chunks):
                upward(me, ch, sent)
                downward(me, ch, sent)
                copy(me, ch, 2, across).wait_send()
                copy(me, ch, 3, sibling).wait_send()

            def sides_sent(slot, ch):
                copy(slot, ch, 2, across).wait_send()
                copy(slot, ch, 3, sibling).wait_send()

            line(lambda slot, ch: None, sent, sent, sides_sent)
            for d in far:
                for ch in range(chunks):
                    copy(lax.rem(across + n - 4 * d, n), ch, 3, sibling).wait_send()

        return finish

    def drain():
        for c in pending:
            c.wait_send()
        pending.clear()

    def pack(value, dst):
        placed[...] = value
        dst[:rows, :] = placed[:, pl.ds(pl.multiple_of(core * shared, 128), step_off)].astype(
            jnp.bfloat16
        )
        half = rows // 2
        folded = placed[:half, pl.ds(mid, shared)] + pltpu.roll(
            placed[half:, pl.ds(mid, shared)], shared // 2, 1
        )
        fold = half * shared // step_off
        for e in range(step_off // shared):
            dst[rows:, e * shared : (e + 1) * shared] = folded[
                e * fold : (e + 1) * fold
            ].astype(jnp.bfloat16)

    low = lax.broadcasted_iota(jnp.int32, (rows // 2, shared), 1) < shared // 2

    def unpack(buf, dst, base, count):
        for p in range(n // 2):
            a, b = buf.at[2 * p], buf.at[2 * p + 1]
            at = p * pair
            half = rows // 2
            dst[pl.ds(base, count), at : at + step_off] = a[:count, :].astype(dst.dtype)
            dst[pl.ds(base, count), at + local : at + pair] = b[:count, :].astype(dst.dtype)
            fa, fb = (
                jnp.concatenate(
                    [
                        r[rows:, e * shared : (e + 1) * shared].astype(jnp.float32)
                        for e in range(step_off // shared)
                    ],
                    axis=0,
                )
                for r in (a, b)
            )
            at = at + step_off
            dst[pl.ds(base, half), at : at + shared] = jnp.where(low, fa, fb).astype(dst.dtype)
            rest = pltpu.roll(jnp.where(low, fb, fa), shared // 2, 1)
            dst[pl.ds(base + half, count - half), at : at + shared] = rest[
                : count - half
            ].astype(dst.dtype)

    lane = lax.broadcasted_iota(jnp.int32, (rows, local), 1)
    shift = core * (local - cols)
    mine = (lane >= shift) & (lane < shift + cols)

    def place(value):
        placed[:, :cols] = value
        placed[:, cols:] = jnp.zeros((rows, local - cols), jnp.float32)
        y = placed[...]
        return jnp.where(mine, jnp.where(core == 1, pltpu.roll(y, local - cols, 1), y), 0.0)

    def assemble(buf, dst, base, count):
        for p in range(n // 2):
            a = buf[2 * p, :count]
            b = buf[2 * p + 1, :count]
            at = p * pair
            kept = pl.ds(base, count)
            dst[kept, at : at + step_off] = a[:, :step_off].astype(dst.dtype)
            dst[kept, at + step_off : at + local] = (
                a[:, step_off:].astype(jnp.float32) + b[:, :shared].astype(jnp.float32)
            ).astype(dst.dtype)
            dst[kept, at + local : at + pair] = b[:, shared:].astype(dst.dtype)

    def modulate():
        def body(i, carry):
            r0 = pl.multiple_of(i * 2 * span, 2 * span)
            c = current[pl.ds(r0, 2 * span), :]
            c = c * lax.rsqrt(jnp.mean(c * c, axis=-1, keepdims=True) + 1e-06)

            def rows_of(kind):
                return jnp.concatenate(
                    [
                        jnp.broadcast_to(mods[kind, pl.ds(2 * i + e, 1), :], (span, width))
                        for e in range(2)
                    ],
                    axis=0,
                )

            full[pl.ds(r0, 2 * span), :] = (c * (1.0 + rows_of(1)) + rows_of(0)).astype(
                jnp.bfloat16
            )
            return carry

        lax.fori_loop(0, n // 2, body, 0)

    qg = q_gain[:, pl.ds(start_col, local)]
    kg = k_gain[:, pl.ds(start_col, local)]
    ones = jnp.ones((8, local), jnp.float32)
    allowed = (
        lax.broadcasted_iota(jnp.int32, (rows, rows), 0) // span
        >= lax.broadcasted_iota(jnp.int32, (rows, rows), 1) // span
    )

    text = []

    def send_text():
        for k in range(1, n):
            target = lax.rem(me + k, n)
            col = pl.multiple_of((target // 2) * pair + lax.rem(target, 2) * step_off, 128)
            for kind, (s, d) in enumerate(((tkeys, tk), (tvals, tv))):
                c = remote(
                    s.at[:, pl.ds(col, local)],
                    d.at[pl.ds(me * trows, trows)],
                    tsend_sems.at[kind, k],
                    trecv_sems.at[kind, me],
                    target,
                )
                c.start()
                text.append(c)

    def prepare():
        send_text()
        own_table.wait()
        picks = (
            lax.broadcasted_iota(jnp.int32, (table.shape[1], n), 0) == levels[...]
        ).astype(jnp.float32)
        picks = jnp.transpose(picks).astype(jnp.bfloat16)
        for kind in range(3):
            mods[kind] = jnp.dot(picks, table[kind], preferred_element_type=jnp.float32)

    part = width // FIRST_CHUNKS
    finish = gather(
        lambda slot, ch: first.at[slot, :, pl.ds(ch * part, part)], FIRST_CHUNKS, 0, prepare
    )
    piece = blocks // CHUNKS

    def block_view(phase):
        return lambda slot, ch: gathered.at[phase, slot, pl.ds(ch * piece, piece)]

    for step in range(STEPS):
        current[0:span, :] = incoming[step].astype(jnp.float32)
        if step == 0:
            for s in range(1, n):
                current[s * span : (s + 1) * span, :] = first[s - 1].astype(jnp.float32)
        else:
            unpack(gathered.at[2 * step - 1], current, span, rows - span)
        modulate()
        if step == 0:
            loads[0].wait()
            loads[1].wait()
        m = full[...]
        q = place(dot_nt(m, wq[...]))
        ssend[step, 0:1] = dot_nt(ones, q * q)[0:1]
        qb[...] = (q * qg).astype(jnp.bfloat16)
        k_ = place(dot_nt(m, wk[...]))
        ssend[step, 1:2] = dot_nt(ones, k_ * k_)[0:1]
        kb[...] = (k_ * kg).astype(jnp.bfloat16)
        for k in range(1, n):
            c = remote(
                ssend.at[step],
                srecv.at[step, me],
                ssend_sems.at[step, k],
                srecv_sems.at[step, me],
                lax.rem(me + k, n),
            )
            c.start()
            pending.append(c)
        srecv[step, me] = ssend[step]
        xsend[step, 0] = qb[:, pl.ds(mid, shared)]
        xsend[step, 1] = kb[:, pl.ds(mid, shared)]
        swap = remote(
            xsend.at[step], xrecv.at[step], xsend_sems.at[step], xrecv_sems.at[step], sibling
        )
        swap.start()
        if step == 0:
            loads[2].wait()
        vb[...] = place(dot_nt(m, wv[...])).astype(
            jnp.bfloat16
        )
        swap.wait()
        qb[:, pl.ds(mid, shared)] = qb[:, pl.ds(mid, shared)] + xrecv[step, 0]
        kb[:, pl.ds(mid, shared)] = kb[:, pl.ds(mid, shared)] + xrecv[step, 1]
        for k in range(1, n):
            src = lax.rem(me + k, n)
            remote(
                ssend.at[step],
                srecv.at[step, src],
                ssend_sems.at[step, k],
                srecv_sems.at[step, src],
                sibling,
            ).wait_recv()
        total = jnp.sum(srecv[step], axis=0)
        inv = lax.rsqrt(total * (1.0 / width) + 1e-06)
        q_col = jnp.transpose(jnp.broadcast_to(inv[0:1], (rows, rows)))[:, 0:1] * scale
        k_row = inv[1:2]
        for h in range(local // head):
            at = slice(h * head, (h + 1) * head)
            s = dot_nt(qb[:, at], kb[:, at]) * q_col * k_row
            s = jnp.where(allowed, s, -1e30)
            w = jnp.exp(s - jnp.max(s, axis=-1, keepdims=True))
            placed[:, at] = jnp.dot(
                w.astype(jnp.bfloat16), vb[:, at], preferred_element_type=jnp.float32
            ) / jnp.sum(w, axis=-1, keepdims=True)
        if step == 0:
            own_tk.wait()
            own_tv.wait()
            for k in range(1, n):
                src = lax.rem(me + k, n)
                for kind, d in enumerate((tk, tv)):
                    remote(
                        d.at[pl.ds(src * trows, trows)],
                        d.at[pl.ds(src * trows, trows)],
                        tsend_sems.at[kind, k],
                        trecv_sems.at[kind, src],
                        sibling,
                    ).wait_recv()
        parts = []
        for h in range(local // head):
            at = slice(h * head, (h + 1) * head)
            t = dot_nt(qb[:, at], tk[:, at]) * q_col
            w = jnp.exp(t - jnp.max(t, axis=-1, keepdims=True))
            b = jnp.dot(
                w.astype(jnp.bfloat16), tv[:, at], preferred_element_type=jnp.float32
            ) / jnp.sum(w, axis=-1, keepdims=True)
            parts.append(placed[:, at] + b)
        pack(
            jnp.where(mine, jnp.concatenate(parts, axis=1), 0.0), gathered.at[2 * step, me]
        )
        finish()
        finish = gather(block_view(2 * step), CHUNKS, 2 * step + 1)
        unpack(gathered.at[2 * step], full, 0, rows)
        if step == 0:
            loads[3].wait()
        projected = place(dot_nt(full[...], wo[...]))
        for s in range(n):
            placed[s * span : (s + 1) * span, :] = jnp.broadcast_to(
                mods[2, s : s + 1, pl.ds(start_col, local)], (span, local)
            )
        state = jnp.where(
            mine, current[:, pl.ds(start_col, local)] + placed[...] * projected, 0.0
        )
        if step < STEPS - 1:
            pack(state, gathered.at[2 * step + 1, me])
            finish()
            finish = gather(block_view(2 * step + 1), CHUNKS, 2 * step + 2)
        else:
            osend[...] = state.reshape(n, span, local).astype(jnp.bfloat16)
            for k in range(1, n):
                target = lax.rem(me + k, n)
                c = remote(
                    osend.at[target],
                    orecv.at[me],
                    osend_sems.at[k],
                    orecv_sems.at[me],
                    target,
                )
                c.start()
                pending.append(c)
            orecv[me] = osend[me]
    for k in range(1, n):
        src = lax.rem(me + k, n)
        remote(
            osend.at[src], orecv.at[src], osend_sems.at[k], orecv_sems.at[src], sibling
        ).wait_recv()
    assemble(orecv, out, 0, span)
    for c in text:
        c.wait_send()
    finish()
    drain()


def per_device_fused(
    hidden,
    incoming,
    levels,
    mod_table,
    query_weight,
    key_weight,
    value_weight,
    output_weight,
    query_gain,
    key_gain,
    text_keys,
    text_values,
):
    n = lax.axis_size("queue")
    span, width = hidden.shape
    cols = query_weight.shape[1]
    head = width // HEADS
    local = -(-cols // head) * head
    shared = 2 * local - 2 * cols
    step_off = 2 * cols - local
    rows = n * span
    text = n * text_keys.shape[0]
    vmem = pl.BlockSpec(memory_space=pltpu.VMEM)
    anywhere = pl.BlockSpec(memory_space=pl.ANY)
    dma = pltpu.SemaphoreType.DMA
    bf16, f32 = jnp.bfloat16, jnp.float32
    weight = pltpu.VMEM((cols, width), bf16)
    most = max(FIRST_CHUNKS, CHUNKS)
    return pl.pallas_call(
        functools.partial(fused_kernel, n, cols),
        out_shape=jax.ShapeDtypeStruct((span, width), hidden.dtype),
        in_specs=[anywhere, vmem, vmem] + [anywhere] * 5 + [vmem] * 2 + [anywhere] * 2,
        out_specs=vmem,
        scratch_shapes=[
            pltpu.VMEM((3, mod_table.shape[0], width), bf16),
            pltpu.VMEM((3, n, width), f32),
            weight,
            weight,
            weight,
            weight,
            pltpu.VMEM((n, span, width), bf16),
            pltpu.VMEM((2 * STEPS - 1, n, rows * cols // step_off, step_off), bf16),
            pltpu.VMEM((rows, width), f32),
            pltpu.VMEM((rows, width), bf16),
            pltpu.VMEM((rows, local), f32),
            pltpu.VMEM((rows, local), bf16),
            pltpu.VMEM((rows, local), bf16),
            pltpu.VMEM((rows, local), bf16),
            pltpu.VMEM((STEPS, 2, rows, shared), bf16),
            pltpu.VMEM((STEPS, 2, rows, shared), bf16),
            pltpu.VMEM((STEPS, 2, rows), f32),
            pltpu.VMEM((STEPS, n, 2, rows), f32),
            pltpu.VMEM((text, local), bf16),
            pltpu.VMEM((text, local), bf16),
            pltpu.VMEM((n, span, local), bf16),
            pltpu.VMEM((n, span, local), bf16),
            dma((8,)),
            dma((2, 4, n, most)),
            dma((2 * STEPS, n, most)),
            dma((STEPS, n)),
            dma((STEPS, n)),
            dma((STEPS,)),
            dma((STEPS,)),
            dma((2, n)),
            dma((2, n)),
            dma((n,)),
            dma((n,)),
        ],
        compiler_params=pltpu.CompilerParams(
            collective_id=0, has_side_effects=True, vmem_limit_bytes=60 * 1024 * 1024
        ),
    )(
        hidden,
        incoming,
        levels.reshape(1, n),
        mod_table.transpose(1, 0, 2),
        query_weight.T,
        key_weight.T,
        value_weight.T,
        output_weight.T,
        query_gain.reshape(1, width),
        key_gain.reshape(1, width),
        text_keys,
        text_values,
    )


def fits_fused(count, rows_total, width, groups):
    head = width // HEADS
    cols = width // count
    span = rows_total // (count * groups)
    return (
        count % 4 == 0
        and head == 128
        and span == 8
        and (2 * cols) % head == 0
        and cols % head == head // 2
        and cols > head
        and count * span == 128
    )


def choose(mesh):
    def run(hidden, incoming, levels, mod_table, *rest):
        count = lax.axis_size("queue")
        if fits_fused(count, hidden.shape[0] * count, hidden.shape[1], 1):
            return per_device_fused(hidden, incoming, levels, mod_table, *rest)
        return per_device(hidden, incoming, levels, mod_table, *rest)

    return run


def solution(mesh):
    in_specs = (
        P(("groups", "queue"), None),
        P(None, "groups", None),
        P(),
        P(),
        P(None, "queue"),
        P(None, "queue"),
        P(None, "queue"),
        P(None, "queue"),
        P(),
        P(),
        P(("groups", "queue"), None),
        P(("groups", "queue"), None),
    )
    out_specs = P(("groups", "queue"), None)
    return jax.shard_map(
        choose(mesh), mesh=mesh, in_specs=in_specs, out_specs=out_specs, check_vma=False
    )
```

profile of v0, /device:TPU:0, one launch (start us, length us, event | category | flops | bytes accessed | tf_op | source)
XLA Modules:
  0.0 103.3 jit_solution(13080446717731867886)
XLA Ops:
  0.0 101.8 %shard_map.118 = bf16[8,5120]{1,0:T(8,128)(2,1)} custom-call(bf16[8,5120]{1,0:T(8,128)(2,1)} %hidden.1, bf16[2,8,5120]{2,1,0:T(8,128)(2,1)} %incoming.1, s32[1,16]{1,0:T(1,128)} %bitcast.15, bf16[3,96,5120]{2,1,0:T(8,128)(2,1)} %bitcast.12, bf16[320,5120]{1,0:T(8,128)(2,1)} %bitcast.8, bf16[320,5120]{1,0:T(8,128)(2,1)} %bitcast.9, ...), custom_call_target="tpu_custom_call" | custom-call | tf_op jit(solution)/shard_map/pallas_call | solution.py:695
  101.8 1.5 %copy.14 = bf16[8,5120]{1,0:T(8,128)(2,1)} copy(bf16[8,5120]{1,0:T(8,128)(2,1)} %shard_map.118) | data formatting | bytes 163840
where the time goes:
time: 104 us; the launch traced here: 103 us
  Pallas kernels  102 us (98%)
  local copies, waits for them, and re-layouts  1.53 us (1%)
    pallas_call x1, Pallas kernels, per_device_fused(): pl.pallas_call(functools.partial(fused_kernel, n, cols), out_shape=jax.Sh...  102 us

commit v1 on v0

--- a/solution.py
+++ b/solution.py
@@ -193,18 +193,24 @@
     out,
     table,
     mods,
-    wq,
-    wk,
-    wv,
+    wqkv,
     wo,
     first,
     gathered,
-    current,
     full,
+    acc,
+    shifted,
+    squares,
+    piece_f32,
+    piece_bf16,
+    oacc,
+    own_cols,
     placed,
     qb,
     kb,
     vb,
+    raw_self,
+    raw_text,
     xsend,
     xrecv,
     ssend,
@@ -234,33 +240,30 @@
     blocks = gathered.shape[2]
     shared = 2 * local - pair
     step_off = pair - local
+    pad = local - cols
     core = lax.rem(me, 2)
+    row = lax.rem(me // 2, 2)
+    depth = me // 4
     sibling = me + 1 - 2 * core
-    across = me + 2 - 4 * lax.rem(me // 2, 2)
-    outer = n // 4
     start_col = pl.multiple_of((me // 2) * pair + core * step_off, 128)
     mid = pl.multiple_of((1 - core) * step_off, 128)
     trows = tkeys.shape[0]
     scale = 1.0 / math.sqrt(head)
 
-    loads = [
-        pltpu.make_async_copy(s, d, load_sems.at[i])
-        for i, (s, d) in enumerate(((wq_hbm, wq), (wk_hbm, wk), (wv_hbm, wv), (wo_hbm, wo)))
-    ]
-    own = pltpu.make_async_copy(hidden, first.at[me], load_sems.at[4])
-    own.start()
-    own_table = pltpu.make_async_copy(table_hbm, table, load_sems.at[7])
-    own_table.start()
-    own_tk = pltpu.make_async_copy(
-        tkeys.at[:, pl.ds(start_col, local)], tk.at[pl.ds(me * trows, trows)], load_sems.at[5]
-    )
-    own_tv = pltpu.make_async_copy(
-        tvals.at[:, pl.ds(start_col, local)], tv.at[pl.ds(me * trows, trows)], load_sems.at[6]
-    )
-    for item in loads + [own_tk, own_tv]:
-        item.start()
-
-    own.wait()
+    upper = depth // 2
+    folded_depth = depth + upper * (3 - 2 * depth)
+
+    def nth(k):
+        x = (folded_depth, 1 - folded_depth, 2, 3)[k]
+        return x + upper * (3 - 2 * x)
+
+    along = [4 * nth(k) + 2 * row + core for k in range(4)]
+    beside = [4 * nth(k) + 2 * (1 - row) + core for k in range(4)]
+    across = me + 2 - 4 * row
+
+    def flip(slot):
+        return slot + 1 - 2 * core
+
     barrier = pltpu.get_barrier_semaphore()
     for k in range(1, n):
         pl.semaphore_signal(
@@ -269,6 +272,35 @@
             device_id={"queue": lax.rem(me + k, n)},
             device_id_type=pl.DeviceIdType.MESH,
         )
+    own = pltpu.make_async_copy(hidden, first.at[me], load_sems.at[4])
+    own.start()
+    own_table = pltpu.make_async_copy(table_hbm, table, load_sems.at[7])
+    own_table.start()
+    blank = jnp.zeros((pad, width), jnp.bfloat16)
+    gap = (1 - core) * cols
+    for j in range(3):
+        wqkv[pl.ds(pl.multiple_of(j * local + gap, pad), pad), :] = blank
+    wo[pl.ds(pl.multiple_of(gap, pad), pad), :] = blank
+    loads = [
+        pltpu.make_async_copy(
+            s, wqkv.at[pl.ds(pl.multiple_of(j * local + core * pad, pad), cols)], load_sems.at[j]
+        )
+        for j, s in enumerate((wq_hbm, wk_hbm, wv_hbm))
+    ]
+    loads.append(
+        pltpu.make_async_copy(
+            wo_hbm, wo.at[pl.ds(pl.multiple_of(core * pad, pad), cols)], load_sems.at[3]
+        )
+    )
+    own_tk = pltpu.make_async_copy(
+        tkeys.at[:, pl.ds(start_col, local)], tk.at[pl.ds(me * trows, trows)], load_sems.at[5]
+    )
+    own_tv = pltpu.make_async_copy(
+        tvals.at[:, pl.ds(start_col, local)], tv.at[pl.ds(me * trows, trows)], load_sems.at[6]
+    )
+    for item in loads + [own_tk, own_tv]:
+        item.start()
+    own.wait()
     pl.semaphore_wait(barrier, n - 1)
 
     pending = []
@@ -283,124 +315,76 @@
             device_id_type=pl.DeviceIdType.MESH,
         )
 
-    def gather(view, chunks, phase, between=None):
+    def gather(view, chunks, phase, on_chip, opening=None, last_link=None):
         bank = phase % 2
-        plane = lax.rem(me, 4)
-        depth = me // 4
+        sent = []
 
         def copy(slot, ch, kind, target):
             return remote(
                 view(slot, ch),
                 view(slot, ch),
-                gsend_sems.at[bank, kind, slot, ch],
+                gsend_sems.at[bank, kind, ch],
                 grecv_sems.at[phase, slot, ch],
                 target,
             )
 
         def push(slot, ch, kind, target):
-            copy(slot, ch, kind, target).start()
+            c = copy(slot, ch, kind, target)
+            c.start()
+            sent.append(c)
 
         def arrived(slot, ch):
-            copy(slot, ch, 3, sibling).wait_recv()
-
-        def upward(slot, ch, act):
-            @pl.when(depth < outer - 1)
-            def _():
-                act(copy(slot, ch, 0, lax.rem(me + 4, n)))
-
-        def downward(slot, ch, act):
-            @pl.when(depth > 0)
-            def _():
-                act(copy(slot, ch, 1, lax.rem(me + n - 4, n)))
-
-        def start(c):
-            c.start()
+            copy(slot, ch, 0, sibling).wait_recv()
 
         for ch in range(chunks):
-            upward(me, ch, start)
-            downward(me, ch, start)
-            push(me, ch, 2, across)
-            push(me, ch, 3, sibling)
-
-        def line(act_in, act_up, act_down, act_side, after=None):
-            for d in range(1, outer):
-                for ch in range(chunks):
-
-                    @pl.when(depth >= d)
-                    def _():
-                        slot = lax.rem(me + n - 4 * d, n)
-                        act_in(slot, ch)
-                        upward(slot, ch, act_up)
-                        act_side(slot, ch)
-
-                    @pl.when(depth < outer - d)
-                    def _():
-                        slot = lax.rem(me + 4 * d, n)
-                        act_in(slot, ch)
-                        downward(slot, ch, act_down)
-                        act_side(slot, ch)
-                if after is not None:
-                    after(d - 1)
-
-        def sides(slot, ch):
-            push(slot, ch, 2, across)
-            push(slot, ch, 3, sibling)
-
-        far = [0] + list(range(1, outer))
-
-        def relay(slot, ch):
-            arrived(slot, ch)
-            push(slot, ch, 3, sibling)
-
-        def other_row(d):
-            if d == outer - 2 and between is not None:
-                between()
+            push(me, ch, 0, across)
+        for k in range(1, 4):
             for ch in range(chunks):
-                if d == 0:
-                    relay(across, ch)
-                else:
-
-                    @pl.when(depth >= d)
-                    def _():
-                        relay(lax.rem(across + n - 4 * d, n), ch)
-
-                    @pl.when(depth < outer - d)
-                    def _():
-                        relay(lax.rem(across + 4 * d, n), ch)
-
-        line(arrived, start, start, sides, other_row)
-        other_row(outer - 1)
-        opposite = me + 3 - 2 * plane
-        for base in (sibling, opposite):
-            for d in far:
-                for ch in range(chunks):
-                    arrived(lax.rem(base + n - 4 * d, n), ch)
-
-        def sent(c):
-            c.wait_send()
+                push(me, ch, k, along[k])
+        for ch in range(chunks):
+            push(me, ch, 4, sibling)
+        if opening is not None:
+            opening()
+
+        def line(k):
+            for ch in range(chunks):
+                arrived(along[k], ch)
+                push(along[k], ch, 4 + k, across)
+                push(along[k], ch, 7 + k, sibling)
+
+        def side(k):
+            for ch in range(chunks):
+                arrived(beside[k], ch)
+                push(beside[k], ch, 11 + k, sibling)
+
+        def chip(slot):
+            for ch in range(chunks):
+                arrived(flip(slot), ch)
+            on_chip(slot // 2)
+
+        line(1)
+        chip(me)
+        side(0)
+        chip(along[1])
+        line(2)
+        chip(beside[0])
+        side(1)
+        chip(along[2])
+        line(3)
+        if last_link is not None:
+            last_link()
+        chip(beside[1])
+        side(2)
+        chip(along[3])
+        side(3)
+        chip(beside[2])
+        chip(beside[3])
 
         def finish():
-            for ch in range(chunks):
-                upward(me, ch, sent)
-                downward(me, ch, sent)
-                copy(me, ch, 2, across).wait_send()
-                copy(me, ch, 3, sibling).wait_send()
-
-            def sides_sent(slot, ch):
-                copy(slot, ch, 2, across).wait_send()
-                copy(slot, ch, 3, sibling).wait_send()
-
-            line(lambda slot, ch: None, sent, sent, sides_sent)
-            for d in far:
-                for ch in range(chunks):
-                    copy(lax.rem(across + n - 4 * d, n), ch, 3, sibling).wait_send()
+            for c in sent:
+                c.wait_send()
 
         return finish
-
-    def drain():
-        for c in pending:
-            c.wait_send()
-        pending.clear()
 
     def pack(value, dst):
         placed[...] = value
@@ -419,39 +403,29 @@
 
     low = lax.broadcasted_iota(jnp.int32, (rows // 2, shared), 1) < shared // 2
 
-    def unpack(buf, dst, base, count):
-        for p in range(n // 2):
-            a, b = buf.at[2 * p], buf.at[2 * p + 1]
-            at = p * pair
-            half = rows // 2
-            dst[pl.ds(base, count), at : at + step_off] = a[:count, :].astype(dst.dtype)
-            dst[pl.ds(base, count), at + local : at + pair] = b[:count, :].astype(dst.dtype)
-            fa, fb = (
-                jnp.concatenate(
-                    [
-                        r[rows:, e * shared : (e + 1) * shared].astype(jnp.float32)
-                        for e in range(step_off // shared)
-                    ],
-                    axis=0,
-                )
-                for r in (a, b)
+    def unpack(buf, chip, dst):
+        a, b = buf.at[2 * chip], buf.at[2 * chip + 1]
+        half = rows // 2
+        dst[:, :step_off] = a[:rows, :].astype(dst.dtype)
+        dst[:, local:pair] = b[:rows, :].astype(dst.dtype)
+        fa, fb = (
+            jnp.concatenate(
+                [
+                    r[rows:, e * shared : (e + 1) * shared].astype(jnp.float32)
+                    for e in range(step_off // shared)
+                ],
+                axis=0,
             )
-            at = at + step_off
-            dst[pl.ds(base, half), at : at + shared] = jnp.where(low, fa, fb).astype(dst.dtype)
-            rest = pltpu.roll(jnp.where(low, fb, fa), shared // 2, 1)
-            dst[pl.ds(base + half, count - half), at : at + shared] = rest[
-                : count - half
-            ].astype(dst.dtype)
+            for r in (a, b)
+        )
+        dst[:half, step_off:local] = jnp.where(low, fa, fb).astype(dst.dtype)
+        dst[half:, step_off:local] = pltpu.roll(jnp.where(low, fb, fa), shared // 2, 1).astype(
+            dst.dtype
+        )
 
     lane = lax.broadcasted_iota(jnp.int32, (rows, local), 1)
-    shift = core * (local - cols)
+    shift = core * pad
     mine = (lane >= shift) & (lane < shift + cols)
-
-    def place(value):
-        placed[:, :cols] = value
-        placed[:, cols:] = jnp.zeros((rows, local - cols), jnp.float32)
-        y = placed[...]
-        return jnp.where(mine, jnp.where(core == 1, pltpu.roll(y, local - cols, 1), y), 0.0)
 
     def assemble(buf, dst, base, count):
         for p in range(n // 2):
@@ -465,35 +439,21 @@
             ).astype(dst.dtype)
             dst[kept, at + local : at + pair] = b[:, shared:].astype(dst.dtype)
 
-    def modulate():
-        def body(i, carry):
-            r0 = pl.multiple_of(i * 2 * span, 2 * span)
-            c = current[pl.ds(r0, 2 * span), :]
-            c = c * lax.rsqrt(jnp.mean(c * c, axis=-1, keepdims=True) + 1e-06)
-
-            def rows_of(kind):
-                return jnp.concatenate(
-                    [
-                        jnp.broadcast_to(mods[kind, pl.ds(2 * i + e, 1), :], (span, width))
-                        for e in range(2)
-                    ],
-                    axis=0,
-                )
-
-            full[pl.ds(r0, 2 * span), :] = (c * (1.0 + rows_of(1)) + rows_of(0)).astype(
-                jnp.bfloat16
-            )
-            return carry
-
-        lax.fori_loop(0, n // 2, body, 0)
+    def spread(ref, at):
+        return jnp.concatenate(
+            [
+                jnp.broadcast_to(ref[(j + 1) % n : (j + 1) % n + 1, at], (span, at.size))
+                for j in range(n)
+            ],
+            axis=0,
+        )
 
     qg = q_gain[:, pl.ds(start_col, local)]
     kg = k_gain[:, pl.ds(start_col, local)]
     ones = jnp.ones((8, local), jnp.float32)
-    allowed = (
-        lax.broadcasted_iota(jnp.int32, (rows, rows), 0) // span
-        >= lax.broadcasted_iota(jnp.int32, (rows, rows), 1) // span
-    )
+    at_row = lax.broadcasted_iota(jnp.int32, (rows, rows), 0) // span
+    at_col = lax.broadcasted_iota(jnp.int32, (rows, rows), 1) // span
+    allowed = lax.rem(at_row + 1, n) >= lax.rem(at_col + 1, n)
 
     text = []
 
@@ -513,42 +473,112 @@
                 text.append(c)
 
     def prepare():
-        send_text()
         own_table.wait()
         picks = (
             lax.broadcasted_iota(jnp.int32, (table.shape[1], n), 0) == levels[...]
         ).astype(jnp.float32)
         picks = jnp.transpose(picks).astype(jnp.bfloat16)
-        for kind in range(3):
-            mods[kind] = jnp.dot(picks, table[kind], preferred_element_type=jnp.float32)
+        drift, gain, gate = (
+            jnp.dot(picks, table[kind], preferred_element_type=jnp.float32) for kind in range(3)
+        )
+        full[rows:, :] = drift.astype(jnp.bfloat16)
+        mods[0] = 1.0 + gain
+        mods[1] = gate
+
+    fresh_row = lax.broadcasted_iota(jnp.int32, (2 * span, 1024), 0) >= span
+
+    def rows_in(chip):
+        at = pl.ds(pl.multiple_of(chip * 2 * span, 2 * span), 2 * span)
+        fresh = fresh_row & (chip == n // 2 - 1)
+        later = lax.rem(2 * chip + 2, n)
+        total = jnp.zeros((2 * span, 128), jnp.float32)
+        for c in range(0, width, 1024):
+            block = slice(c, c + 1024)
+            new = incoming[0, :, block].astype(jnp.float32)
+            x = jnp.concatenate(
+                [
+                    first[2 * chip, :, block].astype(jnp.float32),
+                    first[2 * chip + 1, :, block].astype(jnp.float32),
+                ],
+                axis=0,
+            )
+            x = jnp.where(fresh, jnp.concatenate([new, new], axis=0), x)
+            gain = jnp.concatenate(
+                [
+                    jnp.broadcast_to(mods[0, pl.ds(s, 1), block], (span, 1024))
+                    for s in (2 * chip + 1, later)
+                ],
+                axis=0,
+            )
+            full[at, block] = (x * gain).astype(jnp.bfloat16)
+            y = x * x
+            for e in range(0, 1024, 128):
+                total = total + y[:, e : e + 128]
+        squares[at, :] = total
+
+    def columns_in(step, source):
+        fresh_from = rows - span
+
+        def on_chip(chip):
+            at = pl.ds(pl.multiple_of(chip * pair, 128), pair)
+            unpack(source, chip, piece_f32)
+            piece_f32[fresh_from:, :] = incoming[step, :, at].astype(jnp.float32)
+            x = piece_f32[...]
+            piece_bf16[...] = (x * spread(mods.at[0], at)).astype(jnp.bfloat16)
+            y = x * x
+            total = squares[...]
+            for e in range(0, pair, 128):
+                total = total + y[:, e : e + 128]
+            squares[...] = total
+            acc[...] = acc[...] + dot_nt(piece_bf16[...], wqkv[:, at])
+
+        return on_chip
+
+    def features_in(source):
+        def on_chip(chip):
+            at = pl.ds(pl.multiple_of(chip * pair, 128), pair)
+            unpack(source, chip, piece_bf16)
+            oacc[...] = oacc[...] + dot_nt(piece_bf16[...], wo[:, at])
+
+        return on_chip
 
     part = width // FIRST_CHUNKS
-    finish = gather(
-        lambda slot, ch: first.at[slot, :, pl.ds(ch * part, part)], FIRST_CHUNKS, 0, prepare
-    )
     piece = blocks // CHUNKS
 
     def block_view(phase):
         return lambda slot, ch: gathered.at[phase, slot, pl.ds(ch * piece, piece)]
 
+    own_at = pl.ds(start_col, local)
+    finish = gather(
+        lambda slot, ch: first.at[slot, :, pl.ds(ch * part, part)],
+        FIRST_CHUNKS,
+        0,
+        rows_in,
+        prepare,
+        send_text,
+    )
     for step in range(STEPS):
-        current[0:span, :] = incoming[step].astype(jnp.float32)
         if step == 0:
-            for s in range(1, n):
-                current[s * span : (s + 1) * span, :] = first[s - 1].astype(jnp.float32)
-        else:
-            unpack(gathered.at[2 * step - 1], current, span, rows - span)
-        modulate()
-        if step == 0:
-            loads[0].wait()
-            loads[1].wait()
-        m = full[...]
-        q = place(dot_nt(m, wq[...]))
+            for item in loads[:3]:
+                item.wait()
+            result = dot_nt(full[...], wqkv[...])
+            acc[...] = result[:rows]
+            shifted[...] = result[rows:]
+            for s in range(n - 1):
+                own_cols[s * span : (s + 1) * span, :] = first[s, :, own_at].astype(jnp.float32)
+        own_cols[rows - span :, :] = incoming[step, :, own_at].astype(jnp.float32)
+        r = lax.rsqrt(
+            jnp.sum(squares[...], axis=-1, keepdims=True) * (1.0 / width) + 1e-06
+        )
+
+        def projected_by(j):
+            at = pl.ds(j * local, local)
+            return r * acc[:, at] + spread(shifted, at)
+
+        q = projected_by(0)
         ssend[step, 0:1] = dot_nt(ones, q * q)[0:1]
-        qb[...] = (q * qg).astype(jnp.bfloat16)
-        k_ = place(dot_nt(m, wk[...]))
+        k_ = projected_by(1)
         ssend[step, 1:2] = dot_nt(ones, k_ * k_)[0:1]
-        kb[...] = (k_ * kg).astype(jnp.bfloat16)
         for k in range(1, n):
             c = remote(
                 ssend.at[step],
@@ -559,21 +589,26 @@
             )
             c.start()
             pending.append(c)
-        srecv[step, me] = ssend[step]
+        qb[...] = (q * qg).astype(jnp.bfloat16)
+        kb[...] = (k_ * kg).astype(jnp.bfloat16)
         xsend[step, 0] = qb[:, pl.ds(mid, shared)]
         xsend[step, 1] = kb[:, pl.ds(mid, shared)]
         swap = remote(
             xsend.at[step], xrecv.at[step], xsend_sems.at[step], xrecv_sems.at[step], sibling
         )
         swap.start()
-        if step == 0:
-            loads[2].wait()
-        vb[...] = place(dot_nt(m, wv[...])).astype(
-            jnp.bfloat16
-        )
+        srecv[step, me] = ssend[step]
+        vb[...] = projected_by(2).astype(jnp.bfloat16)
         swap.wait()
         qb[:, pl.ds(mid, shared)] = qb[:, pl.ds(mid, shared)] + xrecv[step, 0]
         kb[:, pl.ds(mid, shared)] = kb[:, pl.ds(mid, shared)] + xrecv[step, 1]
+        for h in range(local // head):
+            at = slice(h * head, (h + 1) * head)
+            raw_self[h] = dot_nt(qb[:, at], kb[:, at])
+        if step > 0:
+            for h in range(local // head):
+                at = slice(h * head, (h + 1) * head)
+                raw_text[h] = dot_nt(qb[:, at], tk[:, at])
         for k in range(1, n):
             src = lax.rem(me + k, n)
             remote(
@@ -589,7 +624,7 @@
         k_row = inv[1:2]
         for h in range(local // head):
             at = slice(h * head, (h + 1) * head)
-            s = dot_nt(qb[:, at], kb[:, at]) * q_col * k_row
+            s = raw_self[h] * q_col * k_row
             s = jnp.where(allowed, s, -1e30)
             w = jnp.exp(s - jnp.max(s, axis=-1, keepdims=True))
             placed[:, at] = jnp.dot(
@@ -598,9 +633,9 @@
         if step == 0:
             own_tk.wait()
             own_tv.wait()
-            for k in range(1, n):
-                src = lax.rem(me + k, n)
-                for kind, d in enumerate((tk, tv)):
+            for kind, d in enumerate((tk, tv)):
+                for k in range(1, n):
+                    src = lax.rem(me + k, n)
                     remote(
                         d.at[pl.ds(src * trows, trows)],
                         d.at[pl.ds(src * trows, trows)],
@@ -608,10 +643,14 @@
                         trecv_sems.at[kind, src],
                         sibling,
                     ).wait_recv()
+                if kind == 0:
+                    for h in range(local // head):
+                        at = slice(h * head, (h + 1) * head)
+                        raw_text[h] = dot_nt(qb[:, at], tk[:, at])
         parts = []
         for h in range(local // head):
             at = slice(h * head, (h + 1) * head)
-            t = dot_nt(qb[:, at], tk[:, at]) * q_col
+            t = raw_text[h] * q_col
             w = jnp.exp(t - jnp.max(t, axis=-1, keepdims=True))
             b = jnp.dot(
                 w.astype(jnp.bfloat16), tv[:, at], preferred_element_type=jnp.float32
@@ -621,22 +660,28 @@
             jnp.where(mine, jnp.concatenate(parts, axis=1), 0.0), gathered.at[2 * step, me]
         )
         finish()
-        finish = gather(block_view(2 * step), CHUNKS, 2 * step + 1)
-        unpack(gathered.at[2 * step], full, 0, rows)
+        oacc[...] = jnp.zeros_like(oacc)
         if step == 0:
             loads[3].wait()
-        projected = place(dot_nt(full[...], wo[...]))
-        for s in range(n):
-            placed[s * span : (s + 1) * span, :] = jnp.broadcast_to(
-                mods[2, s : s + 1, pl.ds(start_col, local)], (span, local)
-            )
+        finish = gather(
+            block_view(2 * step), CHUNKS, 2 * step + 1, features_in(gathered.at[2 * step])
+        )
         state = jnp.where(
-            mine, current[:, pl.ds(start_col, local)] + placed[...] * projected, 0.0
-        )
+            mine, own_cols[...] + spread(mods.at[1], own_at) * oacc[...], 0.0
+        )
+        state = jnp.concatenate([state[rows - span :], state[: rows - span]], axis=0)
         if step < STEPS - 1:
             pack(state, gathered.at[2 * step + 1, me])
             finish()
-            finish = gather(block_view(2 * step + 1), CHUNKS, 2 * step + 2)
+            own_cols[...] = state.astype(jnp.bfloat16).astype(jnp.float32)
+            acc[...] = jnp.zeros_like(acc)
+            squares[...] = jnp.zeros_like(squares)
+            finish = gather(
+                block_view(2 * step + 1),
+                CHUNKS,
+                2 * step + 2,
+                columns_in(step + 1, gathered.at[2 * step + 1]),
+            )
         else:
             osend[...] = state.reshape(n, span, local).astype(jnp.bfloat16)
             for k in range(1, n):
@@ -660,7 +705,8 @@
     for c in text:
         c.wait_send()
     finish()
-    drain()
+    for c in pending:
+        c.wait_send()
 
 
 def per_device_fused(
@@ -684,13 +730,13 @@
     local = -(-cols // head) * head
     shared = 2 * local - 2 * cols
     step_off = 2 * cols - local
+    pair = 2 * cols
     rows = n * span
     text = n * text_keys.shape[0]
     vmem = pl.BlockSpec(memory_space=pltpu.VMEM)
     anywhere = pl.BlockSpec(memory_space=pl.ANY)
     dma = pltpu.SemaphoreType.DMA
     bf16, f32 = jnp.bfloat16, jnp.float32
-    weight = pltpu.VMEM((cols, width), bf16)
     most = max(FIRST_CHUNKS, CHUNKS)
     return pl.pallas_call(
         functools.partial(fused_kernel, n, cols),
@@ -699,19 +745,25 @@
         out_specs=vmem,
         scratch_shapes=[
             pltpu.VMEM((3, mod_table.shape[0], width), bf16),
-            pltpu.VMEM((3, n, width), f32),
-            weight,
-            weight,
-            weight,
-            weight,
+            pltpu.VMEM((2, n, width), f32),
+            pltpu.VMEM((3 * local, width), bf16),
+            pltpu.VMEM((local, width), bf16),
             pltpu.VMEM((n, span, width), bf16),
             pltpu.VMEM((2 * STEPS - 1, n, rows * cols // step_off, step_off), bf16),
-            pltpu.VMEM((rows, width), f32),
-            pltpu.VMEM((rows, width), bf16),
+            pltpu.VMEM((rows + n, width), bf16),
+            pltpu.VMEM((rows, 3 * local), f32),
+            pltpu.VMEM((n, 3 * local), f32),
+            pltpu.VMEM((rows, 128), f32),
+            pltpu.VMEM((rows, pair), f32),
+            pltpu.VMEM((rows, pair), bf16),
+            pltpu.VMEM((rows, local), f32),
+            pltpu.VMEM((rows, local), f32),
             pltpu.VMEM((rows, local), f32),
             pltpu.VMEM((rows, local), bf16),
             pltpu.VMEM((rows, local), bf16),
             pltpu.VMEM((rows, local), bf16),
+            pltpu.VMEM((local // head, rows, rows), f32),
+            pltpu.VMEM((local // head, rows, text), f32),
             pltpu.VMEM((STEPS, 2, rows, shared), bf16),
             pltpu.VMEM((STEPS, 2, rows, shared), bf16),
             pltpu.VMEM((STEPS, 2, rows), f32),
@@ -721,7 +773,7 @@
             pltpu.VMEM((n, span, local), bf16),
             pltpu.VMEM((n, span, local), bf16),
             dma((8,)),
-            dma((2, 4, n, most)),
+            dma((2, 15, most)),
             dma((2 * STEPS, n, most)),
             dma((STEPS, n)),
             dma((STEPS, n)),
@@ -756,7 +808,9 @@
     cols = width // count
     span = rows_total // (count * groups)
     return (
-        count % 4 == 0
+        count // 4 == 4
+        and count % 4 == 0
+        and width % 1024 == 0
         and head == 128
         and span == 8
         and (2 * cols) % head == 0

time: 104 us -> 94 us (0.904)
  Pallas kernels: 102 us -> 92.3 us
    pallas_call x1, Pallas kernels: 102 us -> 92.3 us  [per_device_fused(): pl.pallas_call(functools.partial(fused_kernel, n, cols), out_shape=jax.Sh...]
where the time goes in v1:
time: 94 us; the launch traced here: 93.8 us
  Pallas kernels  92.3 us (98%)
  local copies, waits for them, and re-layouts  1.53 us (2%)
    pallas_call x1, Pallas kernels, per_device_fused(): pl.pallas_call(functools.partial(fused_kernel, n, cols), out_shape=jax.Sh...  92.3 us

profile of v1, /device:TPU:0, one launch (start us, length us, event | category | flops | bytes accessed | tf_op | source)
XLA Modules:
  0.0 93.8 jit_solution(17230039550527092891)
XLA Ops:
  0.0 92.3 %shard_map.118 = bf16[8,5120]{1,0:T(8,128)(2,1)} custom-call(bf16[8,5120]{1,0:T(8,128)(2,1)} %hidden.1, bf16[2,8,5120]{2,1,0:T(8,128)(2,1)} %incoming.1, s32[1,16]{1,0:T(1,128)} %bitcast.15, bf16[3,96,5120]{2,1,0:T(8,128)(2,1)} %bitcast.12, bf16[320,5120]{1,0:T(8,128)(2,1)} %bitcast.8, bf16[320,5120]{1,0:T(8,128)(2,1)} %bitcast.9, ...), custom_call_target="tpu_custom_call" | custom-call | tf_op jit(solution)/shard_map/pallas_call | solution.py:741
  92.3 1.5 %copy.14 = bf16[8,5120]{1,0:T(8,128)(2,1)} copy(bf16[8,5120]{1,0:T(8,128)(2,1)} %shard_map.118) | data formatting | bytes 163840

commit v2 on v1

--- a/solution.py
+++ b/solution.py
@@ -217,6 +217,7 @@
     srecv,
     tk,
     tv,
+    tmid,
     osend,
     orecv,
     load_sems,
@@ -228,6 +229,9 @@
     xrecv_sems,
     tsend_sems,
     trecv_sems,
+    msend_sems,
+    mrecv_sems,
+    msib_sems,
     osend_sems,
     orecv_sems,
 ):
@@ -247,6 +251,8 @@
     sibling = me + 1 - 2 * core
     start_col = pl.multiple_of((me // 2) * pair + core * step_off, 128)
     mid = pl.multiple_of((1 - core) * step_off, 128)
+    mid_start = pl.multiple_of((me // 2) * pair + step_off, 128)
+    own_start = pl.multiple_of((me // 2) * pair + core * local, 128)
     trows = tkeys.shape[0]
     scale = 1.0 / math.sqrt(head)
 
@@ -292,13 +298,27 @@
             wo_hbm, wo.at[pl.ds(pl.multiple_of(core * pad, pad), cols)], load_sems.at[3]
         )
     )
-    own_tk = pltpu.make_async_copy(
-        tkeys.at[:, pl.ds(start_col, local)], tk.at[pl.ds(me * trows, trows)], load_sems.at[5]
-    )
-    own_tv = pltpu.make_async_copy(
-        tvals.at[:, pl.ds(start_col, local)], tv.at[pl.ds(me * trows, trows)], load_sems.at[6]
-    )
-    for item in loads + [own_tk, own_tv]:
+    own_text = [
+        pltpu.make_async_copy(
+            s.at[:, pl.ds(own_start, step_off)], d.at[pl.ds(me * trows, trows)], load_sems.at[5 + i]
+        )
+        for i, (s, d) in enumerate(((tkeys, tk), (tvals, tv)))
+    ]
+
+    def own_middle(kind):
+        return pltpu.make_async_copy(
+            (tkeys, tvals)[kind].at[:, pl.ds(mid_start, shared)],
+            tmid.at[kind, pl.ds(me * trows, trows)],
+            load_sems.at[8],
+        )
+
+    for kind in range(2):
+
+        @pl.when(core == kind)
+        def _():
+            own_middle(kind).start()
+
+    for item in loads + own_text:
         item.start()
     own.wait()
     pl.semaphore_wait(barrier, n - 1)
@@ -315,7 +335,7 @@
             device_id_type=pl.DeviceIdType.MESH,
         )
 
-    def gather(view, chunks, phase, on_chip, opening=None, last_link=None):
+    def gather(view, chunks, phase):
         bank = phase % 2
         sent = []
 
@@ -336,15 +356,14 @@
         def arrived(slot, ch):
             copy(slot, ch, 0, sibling).wait_recv()
 
-        for ch in range(chunks):
-            push(me, ch, 0, across)
-        for k in range(1, 4):
-            for ch in range(chunks):
-                push(me, ch, k, along[k])
-        for ch in range(chunks):
-            push(me, ch, 4, sibling)
-        if opening is not None:
-            opening()
+        def start(some):
+            for ch in some:
+                push(me, ch, 0, across)
+            for k in range(1, 4):
+                for ch in some:
+                    push(me, ch, k, along[k])
+            for ch in some:
+                push(me, ch, 4, sibling)
 
         def line(k):
             for ch in range(chunks):
@@ -357,67 +376,64 @@
                 arrived(beside[k], ch)
                 push(beside[k], ch, 11 + k, sibling)
 
-        def chip(slot):
-            for ch in range(chunks):
-                arrived(flip(slot), ch)
-            on_chip(slot // 2)
-
-        line(1)
-        chip(me)
-        side(0)
-        chip(along[1])
-        line(2)
-        chip(beside[0])
-        side(1)
-        chip(along[2])
-        line(3)
-        if last_link is not None:
-            last_link()
-        chip(beside[1])
-        side(2)
-        chip(along[3])
-        side(3)
-        chip(beside[2])
-        chip(beside[3])
+        def run(on_chip, late=None):
+            def chip(slot, opening=False):
+                for ch in range(chunks):
+                    arrived(flip(slot), ch)
+                on_chip(slot // 2, opening)
+
+            line(1)
+            chip(me, True)
+            side(0)
+            chip(along[1])
+            line(2)
+            chip(beside[0])
+            side(1)
+            chip(along[2])
+            line(3)
+            if late is not None:
+                late()
+            chip(beside[1])
+            side(2)
+            chip(along[3])
+            side(3)
+            chip(beside[2])
+            chip(beside[3])
 
         def finish():
             for c in sent:
                 c.wait_send()
 
-        return finish
-
-    def pack(value, dst):
-        placed[...] = value
-        dst[:rows, :] = placed[:, pl.ds(pl.multiple_of(core * shared, 128), step_off)].astype(
-            jnp.bfloat16
-        )
-        half = rows // 2
-        folded = placed[:half, pl.ds(mid, shared)] + pltpu.roll(
-            placed[half:, pl.ds(mid, shared)], shared // 2, 1
-        )
-        fold = half * shared // step_off
-        for e in range(step_off // shared):
-            dst[rows:, e * shared : (e + 1) * shared] = folded[
-                e * fold : (e + 1) * fold
-            ].astype(jnp.bfloat16)
-
-    low = lax.broadcasted_iota(jnp.int32, (rows // 2, shared), 1) < shared // 2
+        return start, run, finish
+
+    full_heads = step_off // head
+    half = rows // 2
+    low = lax.broadcasted_iota(jnp.int32, (half, shared), 1) < shared // 2
+    owned = (
+        lax.broadcasted_iota(jnp.int32, (rows, shared), 1) // (shared // 2)
+    ) == core
+
+    def head_at(i):
+        if i == full_heads:
+            return pl.ds(mid, head)
+        return pl.ds(pl.multiple_of(core * shared + i * head, 128), head)
+
+    def pack(value, i, dst):
+        if i < full_heads:
+            dst[i * rows : (i + 1) * rows, :] = value.astype(jnp.bfloat16)
+        else:
+            kept = jnp.where(owned, value, 0.0)
+            dst[full_heads * rows :, :] = (
+                kept[:half] + pltpu.roll(kept[half:], shared // 2, 1)
+            ).astype(jnp.bfloat16)
 
     def unpack(buf, chip, dst):
         a, b = buf.at[2 * chip], buf.at[2 * chip + 1]
-        half = rows // 2
-        dst[:, :step_off] = a[:rows, :].astype(dst.dtype)
-        dst[:, local:pair] = b[:rows, :].astype(dst.dtype)
-        fa, fb = (
-            jnp.concatenate(
-                [
-                    r[rows:, e * shared : (e + 1) * shared].astype(jnp.float32)
-                    for e in range(step_off // shared)
-                ],
-                axis=0,
-            )
-            for r in (a, b)
-        )
+        for i in range(full_heads):
+            part = slice(i * rows, (i + 1) * rows)
+            dst[:, i * head : (i + 1) * head] = a[part, :].astype(dst.dtype)
+            dst[:, local + i * head : local + (i + 1) * head] = b[part, :].astype(dst.dtype)
+        fa, fb = (r[full_heads * rows :, :].astype(jnp.float32) for r in (a, b))
         dst[:half, step_off:local] = jnp.where(low, fa, fb).astype(dst.dtype)
         dst[half:, step_off:local] = pltpu.roll(jnp.where(low, fb, fa), shared // 2, 1).astype(
             dst.dtype
@@ -457,20 +473,65 @@
 
     text = []
 
-    def send_text():
+    def send_text(hops):
+        for hop in hops:
+            there = lax.rem(me // 2 + hop, n // 2)
+            base = pl.multiple_of(there * pair, 128)
+            mine_rows = pl.ds(me * trows, trows)
+            copies = [
+                (
+                    e,
+                    remote(
+                        s.at[:, pl.ds(pl.multiple_of(base + step_off, 128), shared)],
+                        tmid.at[e, mine_rows],
+                        msend_sems.at[e, hop],
+                        mrecv_sems.at[me],
+                        2 * there + e,
+                    ),
+                )
+                for e, s in enumerate((tkeys, tvals))
+            ] + [
+                (
+                    e,
+                    remote(
+                        s.at[:, pl.ds(pl.multiple_of(base + e * local, 128), step_off)],
+                        d.at[mine_rows],
+                        tsend_sems.at[kind, e, hop],
+                        trecv_sems.at[kind, me],
+                        2 * there + e,
+                    ),
+                )
+                for kind, (s, d) in enumerate(((tkeys, tk), (tvals, tv)))
+                for e in range(2)
+            ]
+            for e, c in copies:
+                if hop > 0:
+                    c.start()
+                else:
+                    pl.when(core != e)(c.start)
+                text.append((e, hop, c))
+
+    def text_arrived(kind):
+        own_text[kind].wait()
+        d = (tk, tv)[kind]
         for k in range(1, n):
-            target = lax.rem(me + k, n)
-            col = pl.multiple_of((target // 2) * pair + lax.rem(target, 2) * step_off, 128)
-            for kind, (s, d) in enumerate(((tkeys, tk), (tvals, tv))):
-                c = remote(
-                    s.at[:, pl.ds(col, local)],
-                    d.at[pl.ds(me * trows, trows)],
-                    tsend_sems.at[kind, k],
-                    trecv_sems.at[kind, me],
-                    target,
-                )
-                c.start()
-                text.append(c)
+            src = lax.rem(me + k, n)
+            block = d.at[pl.ds(src * trows, trows)]
+            remote(
+                block, block, tsend_sems.at[0, 0, 0], trecv_sems.at[kind, src], sibling
+            ).wait_recv()
+
+    def middle_arrived():
+        own_middle(0).wait()
+        for k in range(1, n):
+            src = lax.rem(me + k, n)
+            block = tmid.at[core, pl.ds(src * trows, trows)]
+            remote(block, block, msend_sems.at[0, 0], mrecv_sems.at[src], sibling).wait_recv()
+
+    def middle(kind):
+        return remote(
+            tmid.at[kind], tmid.at[kind], msib_sems.at[0], msib_sems.at[1], sibling
+        )
 
     def prepare():
         own_table.wait()
@@ -487,7 +548,7 @@
 
     fresh_row = lax.broadcasted_iota(jnp.int32, (2 * span, 1024), 0) >= span
 
-    def rows_in(chip):
+    def rows_in(chip, opening):
         at = pl.ds(pl.multiple_of(chip * 2 * span, 2 * span), 2 * span)
         fresh = fresh_row & (chip == n // 2 - 1)
         later = lax.rem(2 * chip + 2, n)
@@ -519,54 +580,51 @@
     def columns_in(step, source):
         fresh_from = rows - span
 
-        def on_chip(chip):
+        def on_chip(chip, opening):
             at = pl.ds(pl.multiple_of(chip * pair, 128), pair)
             unpack(source, chip, piece_f32)
             piece_f32[fresh_from:, :] = incoming[step, :, at].astype(jnp.float32)
             x = piece_f32[...]
             piece_bf16[...] = (x * spread(mods.at[0], at)).astype(jnp.bfloat16)
             y = x * x
-            total = squares[...]
-            for e in range(0, pair, 128):
+            total = y[:, :128]
+            for e in range(128, pair, 128):
                 total = total + y[:, e : e + 128]
-            squares[...] = total
-            acc[...] = acc[...] + dot_nt(piece_bf16[...], wqkv[:, at])
+            part = dot_nt(piece_bf16[...], wqkv[:, at])
+            squares[...] = total if opening else squares[...] + total
+            acc[...] = part if opening else acc[...] + part
 
         return on_chip
 
     def features_in(source):
-        def on_chip(chip):
+        def on_chip(chip, opening):
             at = pl.ds(pl.multiple_of(chip * pair, 128), pair)
             unpack(source, chip, piece_bf16)
-            oacc[...] = oacc[...] + dot_nt(piece_bf16[...], wo[:, at])
+            part = dot_nt(piece_bf16[...], wo[:, at])
+            oacc[...] = part if opening else oacc[...] + part
 
         return on_chip
 
     part = width // FIRST_CHUNKS
-    piece = blocks // CHUNKS
+    cuts = (0, rows, blocks)
 
     def block_view(phase):
-        return lambda slot, ch: gathered.at[phase, slot, pl.ds(ch * piece, piece)]
+        return lambda slot, ch: gathered.at[phase, slot, pl.ds(cuts[ch], cuts[ch + 1] - cuts[ch])]
 
     own_at = pl.ds(start_col, local)
-    finish = gather(
-        lambda slot, ch: first.at[slot, :, pl.ds(ch * part, part)],
-        FIRST_CHUNKS,
-        0,
-        rows_in,
-        prepare,
-        send_text,
-    )
+    start, run, finish = gather(
+        lambda slot, ch: first.at[slot, :, pl.ds(ch * part, part)], FIRST_CHUNKS, 0
+    )
+    start(range(FIRST_CHUNKS))
+    prepare()
+    run(rows_in, lambda: send_text([2, 4, 6, 1, 3, 5, 7, 0]))
     for step in range(STEPS):
         if step == 0:
-            for item in loads[:3]:
+            for item in loads[:2]:
                 item.wait()
-            result = dot_nt(full[...], wqkv[...])
-            acc[...] = result[:rows]
-            shifted[...] = result[rows:]
-            for s in range(n - 1):
-                own_cols[s * span : (s + 1) * span, :] = first[s, :, own_at].astype(jnp.float32)
-        own_cols[rows - span :, :] = incoming[step, :, own_at].astype(jnp.float32)
+            result = dot_nt(full[...], wqkv[: 2 * local])
+            acc[:, : 2 * local] = result[:rows]
+            shifted[:, : 2 * local] = result[rows:]
         r = lax.rsqrt(
             jnp.sum(squares[...], axis=-1, keepdims=True) * (1.0 / width) + 1e-06
         )
@@ -598,17 +656,25 @@
         )
         swap.start()
         srecv[step, me] = ssend[step]
+        if step == 0:
+            loads[2].wait()
+            result = dot_nt(full[...], wqkv[2 * local :])
+            acc[:, 2 * local :] = result[:rows]
+            shifted[:, 2 * local :] = result[rows:]
+            for s in range(n - 1):
+                own_cols[s * span : (s + 1) * span, :] = first[s, :, own_at].astype(jnp.float32)
+        own_cols[rows - span :, :] = incoming[step, :, own_at].astype(jnp.float32)
         vb[...] = projected_by(2).astype(jnp.bfloat16)
+        for i in range(full_heads):
+            raw_self[i] = dot_nt(qb[:, head_at(i)], kb[:, head_at(i)])
+            if step > 0:
+                raw_text[i] = dot_nt(qb[:, head_at(i)], tk[:, i * head : (i + 1) * head])
         swap.wait()
         qb[:, pl.ds(mid, shared)] = qb[:, pl.ds(mid, shared)] + xrecv[step, 0]
         kb[:, pl.ds(mid, shared)] = kb[:, pl.ds(mid, shared)] + xrecv[step, 1]
-        for h in range(local // head):
-            at = slice(h * head, (h + 1) * head)
-            raw_self[h] = dot_nt(qb[:, at], kb[:, at])
+        raw_self[full_heads] = dot_nt(qb[:, head_at(full_heads)], kb[:, head_at(full_heads)])
         if step > 0:
-            for h in range(local // head):
-                at = slice(h * head, (h + 1) * head)
-                raw_text[h] = dot_nt(qb[:, at], tk[:, at])
+            raw_text[full_heads] = dot_nt(qb[:, head_at(full_heads)], tmid[0])
         for k in range(1, n):
             src = lax.rem(me + k, n)
             remote(
@@ -622,66 +688,64 @@
         inv = lax.rsqrt(total * (1.0 / width) + 1e-06)
         q_col = jnp.transpose(jnp.broadcast_to(inv[0:1], (rows, rows)))[:, 0:1] * scale
         k_row = inv[1:2]
-        for h in range(local // head):
-            at = slice(h * head, (h + 1) * head)
-            s = raw_self[h] * q_col * k_row
+
+        def self_part(i):
+            s = raw_self[i] * q_col * k_row
             s = jnp.where(allowed, s, -1e30)
             w = jnp.exp(s - jnp.max(s, axis=-1, keepdims=True))
-            placed[:, at] = jnp.dot(
-                w.astype(jnp.bfloat16), vb[:, at], preferred_element_type=jnp.float32
+            return jnp.dot(
+                w.astype(jnp.bfloat16), vb[:, head_at(i)], preferred_element_type=jnp.float32
             ) / jnp.sum(w, axis=-1, keepdims=True)
+
+        def text_part(i, values):
+            t = raw_text[i] * q_col
+            w = jnp.exp(t - jnp.max(t, axis=-1, keepdims=True))
+            return jnp.dot(
+                w.astype(jnp.bfloat16), values, preferred_element_type=jnp.float32
+            ) / jnp.sum(w, axis=-1, keepdims=True)
+
         if step == 0:
-            own_tk.wait()
-            own_tv.wait()
-            for kind, d in enumerate((tk, tv)):
-                for k in range(1, n):
-                    src = lax.rem(me + k, n)
-                    remote(
-                        d.at[pl.ds(src * trows, trows)],
-                        d.at[pl.ds(src * trows, trows)],
-                        tsend_sems.at[kind, k],
-                        trecv_sems.at[kind, src],
-                        sibling,
-                    ).wait_recv()
-                if kind == 0:
-                    for h in range(local // head):
-                        at = slice(h * head, (h + 1) * head)
-                        raw_text[h] = dot_nt(qb[:, at], tk[:, at])
-        parts = []
-        for h in range(local // head):
-            at = slice(h * head, (h + 1) * head)
-            t = raw_text[h] * q_col
-            w = jnp.exp(t - jnp.max(t, axis=-1, keepdims=True))
-            b = jnp.dot(
-                w.astype(jnp.bfloat16), tv[:, at], preferred_element_type=jnp.float32
-            ) / jnp.sum(w, axis=-1, keepdims=True)
-            parts.append(placed[:, at] + b)
-        pack(
-            jnp.where(mine, jnp.concatenate(parts, axis=1), 0.0), gathered.at[2 * step, me]
-        )
+            for i in range(full_heads + 1):
+                placed[:, i * head : (i + 1) * head] = self_part(i)
+            middle_arrived()
+            for kind in range(2):
+                pl.when(core == kind)(middle(kind).start)
+            text_arrived(0)
+            for i in range(full_heads):
+                raw_text[i] = dot_nt(qb[:, head_at(i)], tk[:, i * head : (i + 1) * head])
+            text_arrived(1)
+            loads[3].wait()
+        mine_block = gathered.at[2 * step, me]
+        start, run, finish_next = gather(block_view(2 * step), CHUNKS, 2 * step + 1)
+        for i in range(full_heads + 1):
+            if step == 0 and i == full_heads:
+                middle(1 - core).wait_recv()
+                raw_text[i] = dot_nt(qb[:, head_at(i)], tmid[0])
+            values = tv[:, i * head : (i + 1) * head] if i < full_heads else tmid[1]
+            both = placed[:, i * head : (i + 1) * head] if step == 0 else self_part(i)
+            pack(both + text_part(i, values), i, mine_block)
+            if i == 0:
+                start([0])
+        start([1])
         finish()
-        oacc[...] = jnp.zeros_like(oacc)
-        if step == 0:
-            loads[3].wait()
-        finish = gather(
-            block_view(2 * step), CHUNKS, 2 * step + 1, features_in(gathered.at[2 * step])
-        )
+        finish = finish_next
+        run(features_in(gathered.at[2 * step]))
         state = jnp.where(
             mine, own_cols[...] + spread(mods.at[1], own_at) * oacc[...], 0.0
         )
         state = jnp.concatenate([state[rows - span :], state[: rows - span]], axis=0)
         if step < STEPS - 1:
-            pack(state, gathered.at[2 * step + 1, me])
+            placed[...] = state
+            start, run, finish_next = gather(block_view(2 * step + 1), CHUNKS, 2 * step + 2)
+            for i in range(full_heads + 1):
+                pack(placed[:, head_at(i)], i, gathered.at[2 * step + 1, me])
+                if i == 0:
+                    start([0])
+            start([1])
             finish()
+            finish = finish_next
             own_cols[...] = state.astype(jnp.bfloat16).astype(jnp.float32)
-            acc[...] = jnp.zeros_like(acc)
-            squares[...] = jnp.zeros_like(squares)
-            finish = gather(
-                block_view(2 * step + 1),
-                CHUNKS,
-                2 * step + 2,
-                columns_in(step + 1, gathered.at[2 * step + 1]),
-            )
+            run(columns_in(step + 1, gathered.at[2 * step + 1]))
         else:
             osend[...] = state.reshape(n, span, local).astype(jnp.bfloat16)
             for k in range(1, n):
@@ -702,8 +766,12 @@
             osend.at[src], orecv.at[src], osend_sems.at[k], orecv_sems.at[src], sibling
         ).wait_recv()
     assemble(orecv, out, 0, span)
-    for c in text:
-        c.wait_send()
+    for e, hop, c in text:
+        if hop > 0:
+            c.wait_send()
+        else:
+            pl.when(core != e)(c.wait_send)
+    middle(core).wait_send()
     finish()
     for c in pending:
         c.wait_send()
@@ -749,7 +817,7 @@
             pltpu.VMEM((3 * local, width), bf16),
             pltpu.VMEM((local, width), bf16),
             pltpu.VMEM((n, span, width), bf16),
-            pltpu.VMEM((2 * STEPS - 1, n, rows * cols // step_off, step_off), bf16),
+            pltpu.VMEM((2 * STEPS - 1, n, rows * cols // head, head), bf16),
             pltpu.VMEM((rows + n, width), bf16),
             pltpu.VMEM((rows, 3 * local), f32),
             pltpu.VMEM((n, 3 * local), f32),
@@ -768,19 +836,23 @@
             pltpu.VMEM((STEPS, 2, rows, shared), bf16),
             pltpu.VMEM((STEPS, 2, rows), f32),
             pltpu.VMEM((STEPS, n, 2, rows), f32),
-            pltpu.VMEM((text, local), bf16),
-            pltpu.VMEM((text, local), bf16),
+            pltpu.VMEM((text, step_off), bf16),
+            pltpu.VMEM((text, step_off), bf16),
+            pltpu.VMEM((2, text, shared), bf16),
             pltpu.VMEM((n, span, local), bf16),
             pltpu.VMEM((n, span, local), bf16),
-            dma((8,)),
+            dma((9,)),
             dma((2, 15, most)),
             dma((2 * STEPS, n, most)),
             dma((STEPS, n)),
             dma((STEPS, n)),
             dma((STEPS,)),
             dma((STEPS,)),
+            dma((2, 2, n // 2)),
             dma((2, n)),
-            dma((2, n)),
+            dma((2, n // 2)),
+            dma((n,)),
+            dma((2,)),
             dma((n,)),
             dma((n,)),
         ],

time: 94 us -> 91.9 us (0.978)
  Pallas kernels: 92.3 us -> 90.2 us
    pallas_call x1, Pallas kernels: 92.3 us -> 90.2 us  [per_device_fused(): pl.pallas_call(functools.partial(fused_kernel, n, cols), out_shape=jax.Sh...]
where the time goes in v2:
time: 91.9 us; the launch traced here: 91.7 us
  Pallas kernels  90.2 us (98%)
  local copies, waits for them, and re-layouts  1.53 us (2%)
    pallas_call x1, Pallas kernels, per_device_fused(): pl.pallas_call(functools.partial(fused_kernel, n, cols), out_shape=jax.Sh...  90.2 us

profile of v2, /device:TPU:0, one launch (start us, length us, event | category | flops | bytes accessed | tf_op | source)
XLA Modules:
  0.0 91.7 jit_solution(8425290202689878991)
XLA Ops:
  0.0 90.2 %shard_map.118 = bf16[8,5120]{1,0:T(8,128)(2,1)} custom-call(bf16[8,5120]{1,0:T(8,128)(2,1)} %hidden.1, bf16[2,8,5120]{2,1,0:T(8,128)(2,1)} %incoming.1, s32[1,16]{1,0:T(1,128)} %bitcast.15, bf16[3,96,5120]{2,1,0:T(8,128)(2,1)} %bitcast.12, bf16[320,5120]{1,0:T(8,128)(2,1)} %bitcast.8, bf16[320,5120]{1,0:T(8,128)(2,1)} %bitcast.9, ...), custom_call_target="tpu_custom_call" | custom-call | tf_op jit(solution)/shard_map/pallas_call | solution.py:809
  90.2 1.5 %copy.14 = bf16[8,5120]{1,0:T(8,128)(2,1)} copy(bf16[8,5120]{1,0:T(8,128)(2,1)} %shard_map.118) | data formatting | bytes 163840

commit v3 on v2

--- a/solution.py
+++ b/solution.py
@@ -12,6 +12,12 @@
 STEPS = 2
 FIRST_CHUNKS = 2
 CHUNKS = 2
+HALVES_ORDER = (
+    "l10", "s00", "a00", "l20", "a10", "l30", "s10", "b00",
+    "l11", "s01", "a20", "l21", "a01", "s20", "a30", "l31",
+    "b10", "s30", "a11", "s11", "b20", "b30", "h00", "b01",
+    "s21", "a21", "s31", "a31", "b11", "b21", "b31", "h01",
+)
 
 
 def passed_along(value, axis, steps):
@@ -335,15 +341,14 @@
             device_id_type=pl.DeviceIdType.MESH,
         )
 
+    finishes = []
+
     def gather(view, chunks, phase):
-        bank = phase % 2
-        sent = []
-
         def copy(slot, ch, kind, target):
             return remote(
                 view(slot, ch),
                 view(slot, ch),
-                gsend_sems.at[bank, kind, ch],
+                gsend_sems.at[phase, kind, ch],
                 grecv_sems.at[phase, slot, ch],
                 target,
             )
@@ -351,7 +356,7 @@
         def push(slot, ch, kind, target):
             c = copy(slot, ch, kind, target)
             c.start()
-            sent.append(c)
+            finishes.append(c)
 
         def arrived(slot, ch):
             copy(slot, ch, 0, sibling).wait_recv()
@@ -365,52 +370,68 @@
             for ch in some:
                 push(me, ch, 4, sibling)
 
-        def line(k):
-            for ch in range(chunks):
+        def line(k, some):
+            for ch in some:
                 arrived(along[k], ch)
                 push(along[k], ch, 4 + k, across)
                 push(along[k], ch, 7 + k, sibling)
 
-        def side(k):
-            for ch in range(chunks):
+        def side(k, some):
+            for ch in some:
                 arrived(beside[k], ch)
                 push(beside[k], ch, 11 + k, sibling)
 
-        def run(on_chip, late=None):
-            def chip(slot, opening=False):
-                for ch in range(chunks):
+        def run_rows(on_chip, late):
+            every = range(chunks)
+
+            def chip(slot):
+                for ch in every:
                     arrived(flip(slot), ch)
-                on_chip(slot // 2, opening)
-
-            line(1)
-            chip(me, True)
-            side(0)
+                on_chip(slot // 2)
+
+            line(1, every)
+            chip(me)
+            side(0, every)
             chip(along[1])
-            line(2)
+            line(2, every)
             chip(beside[0])
-            side(1)
+            side(1, every)
             chip(along[2])
-            line(3)
-            if late is not None:
-                late()
+            line(3, every)
+            late()
             chip(beside[1])
-            side(2)
+            side(2, every)
             chip(along[3])
-            side(3)
+            side(3, every)
             chip(beside[2])
             chip(beside[3])
 
-        def finish():
-            for c in sent:
-                c.wait_send()
-
-        return start, run, finish
+        def run_halves(on_chip, hook):
+            slots = {"a": along, "b": beside}
+            opened = set()
+            for event in HALVES_ORDER:
+                what, k, half = event[0], int(event[1]), int(event[2])
+                if what == "l":
+                    line(k, [half])
+                elif what == "s":
+                    side(k, [half])
+                elif what == "h":
+                    hook(half)
+                else:
+                    slot = slots[what][k]
+                    arrived(flip(slot), half)
+                    on_chip(slot // 2, half, half not in opened)
+                    opened.add(half)
+
+        return start, run_rows, run_halves
 
     full_heads = step_off // head
-    half = rows // 2
-    low = lax.broadcasted_iota(jnp.int32, (half, shared), 1) < shared // 2
+    half_rows = rows // 2
+    quarter = half_rows // 2
+    half_blocks = blocks // 2
+    low = lax.broadcasted_iota(jnp.int32, (quarter, shared), 1) < shared // 2
     owned = (
-        lax.broadcasted_iota(jnp.int32, (rows, shared), 1) // (shared // 2)
+        lax.broadcasted_iota(jnp.int32, (half_rows, shared), 1) // (shared // 2)
     ) == core
 
     def head_at(i):
@@ -418,28 +439,31 @@
             return pl.ds(mid, head)
         return pl.ds(pl.multiple_of(core * shared + i * head, 128), head)
 
-    def pack(value, i, dst):
+    def pack(value, i, half, dst):
+        base = half * half_blocks + i * half_rows
         if i < full_heads:
-            dst[i * rows : (i + 1) * rows, :] = value.astype(jnp.bfloat16)
+            dst[base : base + half_rows, :] = value.astype(jnp.bfloat16)
         else:
             kept = jnp.where(owned, value, 0.0)
-            dst[full_heads * rows :, :] = (
-                kept[:half] + pltpu.roll(kept[half:], shared // 2, 1)
+            dst[base : base + quarter, :] = (
+                kept[:quarter] + pltpu.roll(kept[quarter:], shared // 2, 1)
             ).astype(jnp.bfloat16)
 
-    def unpack(buf, chip, dst):
+    def unpack(buf, chip, half, dst):
         a, b = buf.at[2 * chip], buf.at[2 * chip + 1]
+        base = half * half_blocks
         for i in range(full_heads):
-            part = slice(i * rows, (i + 1) * rows)
+            part = slice(base + i * half_rows, base + (i + 1) * half_rows)
             dst[:, i * head : (i + 1) * head] = a[part, :].astype(dst.dtype)
             dst[:, local + i * head : local + (i + 1) * head] = b[part, :].astype(dst.dtype)
-        fa, fb = (r[full_heads * rows :, :].astype(jnp.float32) for r in (a, b))
-        dst[:half, step_off:local] = jnp.where(low, fa, fb).astype(dst.dtype)
-        dst[half:, step_off:local] = pltpu.roll(jnp.where(low, fb, fa), shared // 2, 1).astype(
-            dst.dtype
-        )
-
-    lane = lax.broadcasted_iota(jnp.int32, (rows, local), 1)
+        base = base + full_heads * half_rows
+        fa, fb = (r[base : base + quarter, :].astype(jnp.float32) for r in (a, b))
+        dst[:quarter, step_off:local] = jnp.where(low, fa, fb).astype(dst.dtype)
+        dst[quarter:, step_off:local] = pltpu.roll(
+            jnp.where(low, fb, fa), shared // 2, 1
+        ).astype(dst.dtype)
+
+    lane = lax.broadcasted_iota(jnp.int32, (half_rows, local), 1)
     shift = core * pad
     mine = (lane >= shift) & (lane < shift + cols)
 
@@ -455,11 +479,17 @@
             ).astype(dst.dtype)
             dst[kept, at + local : at + pair] = b[:, shared:].astype(dst.dtype)
 
-    def spread(ref, at):
+    def span_of(block, step):
+        return (block + n - STEPS + 1 + step) % n
+
+    def spread(ref, at, step, half):
+        first_block = half * n // 2
         return jnp.concatenate(
             [
-                jnp.broadcast_to(ref[(j + 1) % n : (j + 1) % n + 1, at], (span, at.size))
-                for j in range(n)
+                jnp.broadcast_to(
+                    ref[span_of(i, step) : span_of(i, step) + 1, at], (span, at.size)
+                )
+                for i in range(first_block, first_block + n // 2)
             ],
             axis=0,
         )
@@ -467,9 +497,12 @@
     qg = q_gain[:, pl.ds(start_col, local)]
     kg = k_gain[:, pl.ds(start_col, local)]
     ones = jnp.ones((8, local), jnp.float32)
-    at_row = lax.broadcasted_iota(jnp.int32, (rows, rows), 0) // span
-    at_col = lax.broadcasted_iota(jnp.int32, (rows, rows), 1) // span
-    allowed = lax.rem(at_row + 1, n) >= lax.rem(at_col + 1, n)
+    def causal(step, half, keys):
+        shape = (half_rows, keys)
+        moved = half * n // 2 + n - STEPS + 1 + step
+        at_row = lax.broadcasted_iota(jnp.int32, shape, 0) // span + moved
+        at_col = lax.broadcasted_iota(jnp.int32, shape, 1) // span + n - STEPS + 1 + step
+        return lax.rem(at_row, n) >= lax.rem(at_col, n)
 
     text = []
 
@@ -548,8 +581,9 @@
 
     fresh_row = lax.broadcasted_iota(jnp.int32, (2 * span, 1024), 0) >= span
 
-    def rows_in(chip, opening):
-        at = pl.ds(pl.multiple_of(chip * 2 * span, 2 * span), 2 * span)
+    def rows_in(chip):
+        place = lax.rem(chip + STEPS // 2, n // 2)
+        at = pl.ds(pl.multiple_of(place * 2 * span, 2 * span), 2 * span)
         fresh = fresh_row & (chip == n // 2 - 1)
         later = lax.rem(2 * chip + 2, n)
         total = jnp.zeros((2 * span, 128), jnp.float32)
@@ -577,194 +611,252 @@
                 total = total + y[:, e : e + 128]
         squares[at, :] = total
 
+    def half_at(half):
+        return pl.ds(half * half_rows, half_rows)
+
     def columns_in(step, source):
-        fresh_from = rows - span
-
-        def on_chip(chip, opening):
+        def on_chip(chip, half, opening):
             at = pl.ds(pl.multiple_of(chip * pair, 128), pair)
-            unpack(source, chip, piece_f32)
-            piece_f32[fresh_from:, :] = incoming[step, :, at].astype(jnp.float32)
+            unpack(source, chip, half, piece_f32)
+            if half == 0:
+                piece_f32[:span, :] = incoming[step, :, at].astype(jnp.float32)
             x = piece_f32[...]
-            piece_bf16[...] = (x * spread(mods.at[0], at)).astype(jnp.bfloat16)
+            piece_bf16[...] = (x * spread(mods.at[0], at, step, half)).astype(jnp.bfloat16)
             y = x * x
             total = y[:, :128]
             for e in range(128, pair, 128):
                 total = total + y[:, e : e + 128]
             part = dot_nt(piece_bf16[...], wqkv[:, at])
-            squares[...] = total if opening else squares[...] + total
-            acc[...] = part if opening else acc[...] + part
+            to = half_at(half)
+            squares[to, :] = total if opening else squares[to, :] + total
+            acc[to, :] = part if opening else acc[to, :] + part
 
         return on_chip
 
     def features_in(source):
-        def on_chip(chip, opening):
+        def on_chip(chip, half, opening):
             at = pl.ds(pl.multiple_of(chip * pair, 128), pair)
-            unpack(source, chip, piece_bf16)
+            unpack(source, chip, half, piece_bf16)
             part = dot_nt(piece_bf16[...], wo[:, at])
-            oacc[...] = part if opening else oacc[...] + part
+            to = half_at(half)
+            oacc[to, :] = part if opening else oacc[to, :] + part
 
         return on_chip
 
     part = width // FIRST_CHUNKS
-    cuts = (0, rows, blocks)
 
     def block_view(phase):
-        return lambda slot, ch: gathered.at[phase, slot, pl.ds(cuts[ch], cuts[ch + 1] - cuts[ch])]
+        return lambda slot, ch: gathered.at[phase, slot, pl.ds(ch * half_blocks, half_blocks)]
 
     own_at = pl.ds(start_col, local)
-    start, run, finish = gather(
+
+    def norm_copy(turn, k, src, target):
+        return remote(
+            ssend.at[turn],
+            srecv.at[turn, src],
+            ssend_sems.at[turn, k],
+            srecv_sems.at[turn, src],
+            target,
+        )
+
+    def swap_copy(turn):
+        return remote(
+            xsend.at[turn], xrecv.at[turn], xsend_sems.at[turn], xrecv_sems.at[turn], sibling
+        )
+
+    def projected_by(j, step, half):
+        at = pl.ds(j * local, local)
+        to = half_at(half)
+        r = lax.rsqrt(
+            jnp.sum(squares[to, :], axis=-1, keepdims=True) * (1.0 / width) + 1e-06
+        )
+        return r * acc[to, at] + spread(shifted, at, step, half)
+
+    def square_sums(value):
+        sums = dot_nt(ones, value * value)[0:1]
+        return jnp.concatenate([sums, sums], axis=1)
+
+    def launch(step, half):
+        turn = 2 * step + half
+        to = half_at(half)
+        q = projected_by(0, step, half)
+        ssend[turn, 0:1] = square_sums(q)
+        k_ = projected_by(1, step, half)
+        ssend[turn, 1:2] = square_sums(k_)
+        for k in range(1, n):
+            c = norm_copy(turn, k, me, lax.rem(me + k, n))
+            c.start()
+            pending.append(c)
+        qb[to, :] = (q * qg).astype(jnp.bfloat16)
+        kb[to, :] = (k_ * kg).astype(jnp.bfloat16)
+        xsend[turn, 0] = qb[to, pl.ds(mid, shared)]
+        xsend[turn, 1] = kb[to, pl.ds(mid, shared)]
+        swap_copy(turn).start()
+        srecv[turn, me] = ssend[turn]
+
+    def swapped(turn, half):
+        to = half_at(half)
+        swap_copy(turn).wait()
+        qb[to, pl.ds(mid, shared)] = qb[to, pl.ds(mid, shared)] + xrecv[turn, 0]
+        kb[to, pl.ds(mid, shared)] = kb[to, pl.ds(mid, shared)] + xrecv[turn, 1]
+
+    k_rows = {}
+
+    def norms_arrived(turn):
+        for k in range(1, n):
+            norm_copy(turn, k, lax.rem(me + k, n), sibling).wait_recv()
+        inv = lax.rsqrt(jnp.sum(srecv[turn], axis=0) * (1.0 / width) + 1e-06)
+        k_rows[turn] = inv[1:2]
+        turned = jnp.transpose(jnp.broadcast_to(inv[0:1], (rows, rows)))
+        return turned[:half_rows, 0:1] * scale
+
+    def keys_of(step, half):
+        return rows if step == 0 or half == 1 else half_rows
+
+    def score_self(i, step, half):
+        keys = keys_of(step, half)
+        to = half_at(half)
+        raw_self[i, to, :keys] = dot_nt(qb[to, head_at(i)], kb[:keys, head_at(i)])
+
+    def score_text(i, half):
+        keys = tk[:, i * head : (i + 1) * head] if i < full_heads else tmid[0]
+        to = half_at(half)
+        raw_text[i, to, :] = dot_nt(qb[to, head_at(i)], keys)
+
+    low_keys = lax.broadcasted_iota(jnp.int32, (1, rows), 1) < half_rows
+
+    def self_part(i, step, half, q_col):
+        keys = keys_of(step, half)
+        if keys == rows:
+            k_row = jnp.where(low_keys, k_rows[2 * step], k_rows[2 * step + 1])
+        else:
+            k_row = k_rows[2 * step][:, :keys]
+        s = raw_self[i, half_at(half), :keys] * q_col * k_row
+        s = jnp.where(causal(step, half, keys), s, -1e30)
+        w = jnp.exp(s - jnp.max(s, axis=-1, keepdims=True))
+        return jnp.dot(
+            w.astype(jnp.bfloat16), vb[:keys, head_at(i)], preferred_element_type=jnp.float32
+        ) / jnp.sum(w, axis=-1, keepdims=True)
+
+    def text_part(i, half, q_col):
+        values = tv[:, i * head : (i + 1) * head] if i < full_heads else tmid[1]
+        t = raw_text[i, half_at(half), :] * q_col
+        w = jnp.exp(t - jnp.max(t, axis=-1, keepdims=True))
+        return jnp.dot(
+            w.astype(jnp.bfloat16), values, preferred_element_type=jnp.float32
+        ) / jnp.sum(w, axis=-1, keepdims=True)
+
+    def state_of(step, half):
+        to = half_at(half)
+        gate = spread(mods.at[1], own_at, step, half)
+        return jnp.where(mine, own_cols[to, :] + gate * oacc[to, :], 0.0)
+
+    def final_copy(src, dst, target):
+        return remote(
+            osend.at[src], orecv.at[dst], osend_sems.at[src], orecv_sems.at[dst], target
+        )
+
+    every_head = range(full_heads + 1)
+    start, run_rows, _ = gather(
         lambda slot, ch: first.at[slot, :, pl.ds(ch * part, part)], FIRST_CHUNKS, 0
     )
     start(range(FIRST_CHUNKS))
     prepare()
-    run(rows_in, lambda: send_text([2, 4, 6, 1, 3, 5, 7, 0]))
+    run_rows(rows_in, lambda: send_text([2, 4, 6, 1, 3, 5, 7, 0]))
+    for item in loads[:2]:
+        item.wait()
+    result = dot_nt(full[...], wqkv[: 2 * local])
+    acc[:, : 2 * local] = result[:rows]
+    shifted[:, : 2 * local] = result[rows:]
+    for half in range(2):
+        launch(0, half)
+    loads[2].wait()
+    result = dot_nt(full[...], wqkv[2 * local :])
+    acc[:, 2 * local :] = result[:rows]
+    shifted[:, 2 * local :] = result[rows:]
+    for i in range(n):
+        rows_of = slice(i * span, (i + 1) * span)
+        if i == STEPS - 1:
+            own_cols[rows_of, :] = incoming[0, :, own_at].astype(jnp.float32)
+        else:
+            own_cols[rows_of, :] = first[(i - STEPS) % n, :, own_at].astype(jnp.float32)
+    for half in range(2):
+        vb[half_at(half), :] = projected_by(2, 0, half).astype(jnp.bfloat16)
+        swapped(half, half)
+    for half in range(2):
+        for i in every_head:
+            score_self(i, 0, half)
+    q_cols = [norms_arrived(half) for half in range(2)]
+    for half in range(2):
+        for i in every_head:
+            placed[half_at(half), i * head : (i + 1) * head] = self_part(i, 0, half, q_cols[half])
+    middle_arrived()
+    for kind in range(2):
+        pl.when(core == kind)(middle(kind).start)
+    text_arrived(0)
+    for half in range(2):
+        for i in range(full_heads):
+            score_text(i, half)
+    text_arrived(1)
+    loads[3].wait()
+    middle(1 - core).wait_recv()
+    start, _, run_halves = gather(block_view(0), CHUNKS, 1)
+    for half in range(2):
+        score_text(full_heads, half)
+        for i in every_head:
+            both = placed[half_at(half), i * head : (i + 1) * head] + text_part(
+                i, half, q_cols[half]
+            )
+            pack(both, i, half, gathered.at[0, me])
+        start([half])
+
     for step in range(STEPS):
-        if step == 0:
-            for item in loads[:2]:
-                item.wait()
-            result = dot_nt(full[...], wqkv[: 2 * local])
-            acc[:, : 2 * local] = result[:rows]
-            shifted[:, : 2 * local] = result[rows:]
-        r = lax.rsqrt(
-            jnp.sum(squares[...], axis=-1, keepdims=True) * (1.0 / width) + 1e-06
-        )
-
-        def projected_by(j):
-            at = pl.ds(j * local, local)
-            return r * acc[:, at] + spread(shifted, at)
-
-        q = projected_by(0)
-        ssend[step, 0:1] = dot_nt(ones, q * q)[0:1]
-        k_ = projected_by(1)
-        ssend[step, 1:2] = dot_nt(ones, k_ * k_)[0:1]
-        for k in range(1, n):
-            c = remote(
-                ssend.at[step],
-                srecv.at[step, me],
-                ssend_sems.at[step, k],
-                srecv_sems.at[step, me],
-                lax.rem(me + k, n),
-            )
-            c.start()
-            pending.append(c)
-        qb[...] = (q * qg).astype(jnp.bfloat16)
-        kb[...] = (k_ * kg).astype(jnp.bfloat16)
-        xsend[step, 0] = qb[:, pl.ds(mid, shared)]
-        xsend[step, 1] = kb[:, pl.ds(mid, shared)]
-        swap = remote(
-            xsend.at[step], xrecv.at[step], xsend_sems.at[step], xrecv_sems.at[step], sibling
-        )
-        swap.start()
-        srecv[step, me] = ssend[step]
-        if step == 0:
-            loads[2].wait()
-            result = dot_nt(full[...], wqkv[2 * local :])
-            acc[:, 2 * local :] = result[:rows]
-            shifted[:, 2 * local :] = result[rows:]
-            for s in range(n - 1):
-                own_cols[s * span : (s + 1) * span, :] = first[s, :, own_at].astype(jnp.float32)
-        own_cols[rows - span :, :] = incoming[step, :, own_at].astype(jnp.float32)
-        vb[...] = projected_by(2).astype(jnp.bfloat16)
-        for i in range(full_heads):
-            raw_self[i] = dot_nt(qb[:, head_at(i)], kb[:, head_at(i)])
-            if step > 0:
-                raw_text[i] = dot_nt(qb[:, head_at(i)], tk[:, i * head : (i + 1) * head])
-        swap.wait()
-        qb[:, pl.ds(mid, shared)] = qb[:, pl.ds(mid, shared)] + xrecv[step, 0]
-        kb[:, pl.ds(mid, shared)] = kb[:, pl.ds(mid, shared)] + xrecv[step, 1]
-        raw_self[full_heads] = dot_nt(qb[:, head_at(full_heads)], kb[:, head_at(full_heads)])
-        if step > 0:
-            raw_text[full_heads] = dot_nt(qb[:, head_at(full_heads)], tmid[0])
-        for k in range(1, n):
-            src = lax.rem(me + k, n)
-            remote(
-                ssend.at[step],
-                srecv.at[step, src],
-                ssend_sems.at[step, k],
-                srecv_sems.at[step, src],
-                sibling,
-            ).wait_recv()
-        total = jnp.sum(srecv[step], axis=0)
-        inv = lax.rsqrt(total * (1.0 / width) + 1e-06)
-        q_col = jnp.transpose(jnp.broadcast_to(inv[0:1], (rows, rows)))[:, 0:1] * scale
-        k_row = inv[1:2]
-
-        def self_part(i):
-            s = raw_self[i] * q_col * k_row
-            s = jnp.where(allowed, s, -1e30)
-            w = jnp.exp(s - jnp.max(s, axis=-1, keepdims=True))
-            return jnp.dot(
-                w.astype(jnp.bfloat16), vb[:, head_at(i)], preferred_element_type=jnp.float32
-            ) / jnp.sum(w, axis=-1, keepdims=True)
-
-        def text_part(i, values):
-            t = raw_text[i] * q_col
-            w = jnp.exp(t - jnp.max(t, axis=-1, keepdims=True))
-            return jnp.dot(
-                w.astype(jnp.bfloat16), values, preferred_element_type=jnp.float32
-            ) / jnp.sum(w, axis=-1, keepdims=True)
-
-        if step == 0:
-            for i in range(full_heads + 1):
-                placed[:, i * head : (i + 1) * head] = self_part(i)
-            middle_arrived()
-            for kind in range(2):
-                pl.when(core == kind)(middle(kind).start)
-            text_arrived(0)
-            for i in range(full_heads):
-                raw_text[i] = dot_nt(qb[:, head_at(i)], tk[:, i * head : (i + 1) * head])
-            text_arrived(1)
-            loads[3].wait()
-        mine_block = gathered.at[2 * step, me]
-        start, run, finish_next = gather(block_view(2 * step), CHUNKS, 2 * step + 1)
-        for i in range(full_heads + 1):
-            if step == 0 and i == full_heads:
-                middle(1 - core).wait_recv()
-                raw_text[i] = dot_nt(qb[:, head_at(i)], tmid[0])
-            values = tv[:, i * head : (i + 1) * head] if i < full_heads else tmid[1]
-            both = placed[:, i * head : (i + 1) * head] if step == 0 else self_part(i)
-            pack(both + text_part(i, values), i, mine_block)
-            if i == 0:
-                start([0])
-        start([1])
-        finish()
-        finish = finish_next
-        run(features_in(gathered.at[2 * step]))
-        state = jnp.where(
-            mine, own_cols[...] + spread(mods.at[1], own_at) * oacc[...], 0.0
-        )
-        state = jnp.concatenate([state[rows - span :], state[: rows - span]], axis=0)
-        if step < STEPS - 1:
-            placed[...] = state
-            start, run, finish_next = gather(block_view(2 * step + 1), CHUNKS, 2 * step + 2)
-            for i in range(full_heads + 1):
-                pack(placed[:, head_at(i)], i, gathered.at[2 * step + 1, me])
-                if i == 0:
-                    start([0])
-            start([1])
-            finish()
-            finish = finish_next
-            own_cols[...] = state.astype(jnp.bfloat16).astype(jnp.float32)
-            run(columns_in(step + 1, gathered.at[2 * step + 1]))
-        else:
-            osend[...] = state.reshape(n, span, local).astype(jnp.bfloat16)
-            for k in range(1, n):
-                target = lax.rem(me + k, n)
-                c = remote(
-                    osend.at[target],
-                    orecv.at[me],
-                    osend_sems.at[k],
-                    orecv_sems.at[me],
-                    target,
-                )
-                c.start()
-                pending.append(c)
-            orecv[me] = osend[me]
+        last = step == STEPS - 1
+        if not last:
+            start_next, _, run_next = gather(block_view(2 * step + 1), CHUNKS, 2 * step + 2)
+
+        def features_done(half):
+            state = state_of(step, half)
+            if last:
+                spans = slice(half * n // 2, (half + 1) * n // 2)
+                osend[spans] = state.reshape(n // 2, span, local).astype(jnp.bfloat16)
+                for target in range(half * n // 2, (half + 1) * n // 2):
+                    pl.when(me != target)(final_copy(target, me, target).start)
+                return
+            placed[half_at(half), :] = state
+            for i in every_head:
+                pack(placed[half_at(half), head_at(i)], i, half, gathered.at[2 * step + 1, me])
+            start_next([half])
+            own_cols[half_at(half), :] = state.astype(jnp.bfloat16).astype(jnp.float32)
+            if half == 0:
+                fresh = slice((STEPS - 2 - step) * span, (STEPS - 1 - step) * span)
+                own_cols[fresh, :] = incoming[step + 1, :, own_at].astype(jnp.float32)
+
+        run_halves(features_in(gathered.at[2 * step]), features_done)
+        if last:
+            break
+
+        def columns_done(half):
+            launch(step + 1, half)
+            vb[half_at(half), :] = projected_by(2, step + 1, half).astype(jnp.bfloat16)
+
+        run_next(columns_in(step + 1, gathered.at[2 * step + 1]), columns_done)
+        start, _, run_halves = gather(block_view(2 * step + 2), CHUNKS, 2 * step + 3)
+        for half in range(2):
+            turn = 2 * (step + 1) + half
+            swapped(turn, half)
+            for i in every_head:
+                score_self(i, step + 1, half)
+                score_text(i, half)
+            q_col = norms_arrived(turn)
+            for i in every_head:
+                both = self_part(i, step + 1, half, q_col) + text_part(i, half, q_col)
+                pack(both, i, half, gathered.at[2 * step + 2, me])
+            start([half])
+    orecv[me] = osend[me]
     for k in range(1, n):
         src = lax.rem(me + k, n)
-        remote(
-            osend.at[src], orecv.at[src], osend_sems.at[k], orecv_sems.at[src], sibling
-        ).wait_recv()
+        final_copy(src, src, sibling).wait_recv()
     assemble(orecv, out, 0, span)
     for e, hop, c in text:
         if hop > 0:
@@ -772,8 +864,9 @@
         else:
             pl.when(core != e)(c.wait_send)
     middle(core).wait_send()
-    finish()
-    for c in pending:
+    for target in range(n):
+        pl.when(me != target)(final_copy(target, me, target).wait_send)
+    for c in finishes + pending:
         c.wait_send()
 
 
@@ -822,8 +915,8 @@
             pltpu.VMEM((rows, 3 * local), f32),
             pltpu.VMEM((n, 3 * local), f32),
             pltpu.VMEM((rows, 128), f32),
-            pltpu.VMEM((rows, pair), f32),
-            pltpu.VMEM((rows, pair), bf16),
+            pltpu.VMEM((rows // 2, pair), f32),
+            pltpu.VMEM((rows // 2, pair), bf16),
             pltpu.VMEM((rows, local), f32),
             pltpu.VMEM((rows, local), f32),
             pltpu.VMEM((rows, local), f32),
@@ -832,22 +925,22 @@
             pltpu.VMEM((rows, local), bf16),
             pltpu.VMEM((local // head, rows, rows), f32),
             pltpu.VMEM((local // head, rows, text), f32),
-            pltpu.VMEM((STEPS, 2, rows, shared), bf16),
-            pltpu.VMEM((STEPS, 2, rows, shared), bf16),
-            pltpu.VMEM((STEPS, 2, rows), f32),
-            pltpu.VMEM((STEPS, n, 2, rows), f32),
+            pltpu.VMEM((2 * STEPS, 2, rows // 2, shared), bf16),
+            pltpu.VMEM((2 * STEPS, 2, rows // 2, shared), bf16),
+            pltpu.VMEM((2 * STEPS, 2, rows), f32),
+            pltpu.VMEM((2 * STEPS, n, 2, rows), f32),
             pltpu.VMEM((text, step_off), bf16),
             pltpu.VMEM((text, step_off), bf16),
             pltpu.VMEM((2, text, shared), bf16),
             pltpu.VMEM((n, span, local), bf16),
             pltpu.VMEM((n, span, local), bf16),
             dma((9,)),
-            dma((2, 15, most)),
+            dma((2 * STEPS, 15, most)),
             dma((2 * STEPS, n, most)),
-            dma((STEPS, n)),
-            dma((STEPS, n)),
-            dma((STEPS,)),
-            dma((STEPS,)),
+            dma((2 * STEPS, n)),
+            dma((2 * STEPS, n)),
+            dma((2 * STEPS,)),
+            dma((2 * STEPS,)),
             dma((2, 2, n // 2)),
             dma((2, n)),
             dma((2, n // 2)),

time: 91.9 us -> 88.5 us (0.963)
  Pallas kernels: 90.2 us -> 86.8 us
    pallas_call x1, Pallas kernels: 90.2 us -> 86.8 us  [per_device_fused(): pl.pallas_call(functools.partial(fused_kernel, n, cols), out_shape=jax.Sh...]
where the time goes in v3:
time: 88.5 us; the launch traced here: 88.3 us
  Pallas kernels  86.8 us (98%)
  local copies, waits for them, and re-layouts  1.53 us (2%)
    pallas_call x1, Pallas kernels, per_device_fused(): pl.pallas_call(functools.partial(fused_kernel, n, cols), out_shape=jax.Sh...  86.8 us

profile of v3, /device:TPU:0, one launch (start us, length us, event | category | flops | bytes accessed | tf_op | source)
XLA Modules:
  0.0 88.3 jit_solution(6286323340442378363)
XLA Ops:
  0.0 86.8 %shard_map.118 = bf16[8,5120]{1,0:T(8,128)(2,1)} custom-call(bf16[8,5120]{1,0:T(8,128)(2,1)} %hidden.1, bf16[2,8,5120]{2,1,0:T(8,128)(2,1)} %incoming.1, s32[1,16]{1,0:T(1,128)} %bitcast.15, bf16[3,96,5120]{2,1,0:T(8,128)(2,1)} %bitcast.12, bf16[320,5120]{1,0:T(8,128)(2,1)} %bitcast.8, bf16[320,5120]{1,0:T(8,128)(2,1)} %bitcast.9, ...), custom_call_target="tpu_custom_call" | custom-call | tf_op jit(solution)/shard_map/pallas_call | solution.py:902
  86.8 1.5 %copy.14 = bf16[8,5120]{1,0:T(8,128)(2,1)} copy(bf16[8,5120]{1,0:T(8,128)(2,1)} %shard_map.118) | data formatting | bytes 163840

commit v4 on v3

--- a/solution.py
+++ b/solution.py
@@ -201,6 +201,8 @@
     mods,
     wqkv,
     wo,
+    wqkv_t,
+    wo_t,
     first,
     gathered,
     full,
@@ -384,10 +386,13 @@
         def run_rows(on_chip, late):
             every = range(chunks)
 
+            counts = iter(range(n // 2))
+
             def chip(slot):
                 for ch in every:
                     arrived(flip(slot), ch)
                 on_chip(slot // 2)
+                turn_over_between(next(counts))
 
             line(1, every)
             chip(me)
@@ -611,6 +616,22 @@
                 total = total + y[:, e : e + 128]
         squares[at, :] = total
 
+    def turn_over(source, target, lines, chunk):
+        at = slice(chunk * pair, (chunk + 1) * pair)
+        target[at, lines] = source[lines, at].T
+
+    both_kinds, last_kind = slice(0, 2 * local), slice(2 * local, 3 * local)
+    chunk_total = n // 2
+
+    def turn_over_between(count):
+        early = chunk_total // 2
+        if count == early:
+            loads[2].wait()
+        if early <= count < early + 2:
+            for chunk in range(chunk_total):
+                if chunk % 2 == count - early:
+                    turn_over(wqkv, wqkv_t, last_kind, chunk)
+
     def half_at(half):
         return pl.ds(half * half_rows, half_rows)
 
@@ -626,7 +647,9 @@
             total = y[:, :128]
             for e in range(128, pair, 128):
                 total = total + y[:, e : e + 128]
-            part = dot_nt(piece_bf16[...], wqkv[:, at])
+            part = jnp.dot(
+                piece_bf16[...], wqkv_t[at, :], preferred_element_type=jnp.float32
+            )
             to = half_at(half)
             squares[to, :] = total if opening else squares[to, :] + total
             acc[to, :] = part if opening else acc[to, :] + part
@@ -637,7 +660,7 @@
         def on_chip(chip, half, opening):
             at = pl.ds(pl.multiple_of(chip * pair, 128), pair)
             unpack(source, chip, half, piece_bf16)
-            part = dot_nt(piece_bf16[...], wo[:, at])
+            part = jnp.dot(piece_bf16[...], wo_t[at, :], preferred_element_type=jnp.float32)
             to = half_at(half)
             oacc[to, :] = part if opening else oacc[to, :] + part
 
@@ -762,16 +785,17 @@
     )
     start(range(FIRST_CHUNKS))
     prepare()
-    run_rows(rows_in, lambda: send_text([2, 4, 6, 1, 3, 5, 7, 0]))
     for item in loads[:2]:
         item.wait()
-    result = dot_nt(full[...], wqkv[: 2 * local])
+    for chunk in range(chunk_total):
+        turn_over(wqkv, wqkv_t, both_kinds, chunk)
+    run_rows(rows_in, lambda: send_text([2, 4, 6, 1, 3, 5, 7, 0]))
+    result = jnp.dot(full[...], wqkv_t[:, both_kinds], preferred_element_type=jnp.float32)
     acc[:, : 2 * local] = result[:rows]
     shifted[:, : 2 * local] = result[rows:]
     for half in range(2):
         launch(0, half)
-    loads[2].wait()
-    result = dot_nt(full[...], wqkv[2 * local :])
+    result = jnp.dot(full[...], wqkv_t[:, last_kind], preferred_element_type=jnp.float32)
     acc[:, 2 * local :] = result[:rows]
     shifted[:, 2 * local :] = result[rows:]
     for i in range(n):
@@ -786,6 +810,9 @@
     for half in range(2):
         for i in every_head:
             score_self(i, 0, half)
+    loads[3].wait()
+    for chunk in range(chunk_total):
+        turn_over(wo, wo_t, slice(0, local), chunk)
     q_cols = [norms_arrived(half) for half in range(2)]
     for half in range(2):
         for i in every_head:
@@ -798,7 +825,6 @@
         for i in range(full_heads):
             score_text(i, half)
     text_arrived(1)
-    loads[3].wait()
     middle(1 - core).wait_recv()
     start, _, run_halves = gather(block_view(0), CHUNKS, 1)
     for half in range(2):
@@ -909,6 +935,8 @@
             pltpu.VMEM((2, n, width), f32),
             pltpu.VMEM((3 * local, width), bf16),
             pltpu.VMEM((local, width), bf16),
+            pltpu.VMEM((width, 3 * local), bf16),
+            pltpu.VMEM((width, local), bf16),
             pltpu.VMEM((n, span, width), bf16),
             pltpu.VMEM((2 * STEPS - 1, n, rows * cols // head, head), bf16),
             pltpu.VMEM((rows + n, width), bf16),

time: 88.5 us -> 85.5 us (0.966)
  Pallas kernels: 86.8 us -> 83.8 us
    pallas_call x1, Pallas kernels: 86.8 us -> 83.8 us  [per_device_fused(): pl.pallas_call(functools.partial(fused_kernel, n, cols), out_shape=jax.Sh...]
where the time goes in v4:
time: 85.5 us; the launch traced here: 85.3 us
  Pallas kernels  83.8 us (98%)
  local copies, waits for them, and re-layouts  1.53 us (2%)
    pallas_call x1, Pallas kernels, per_device_fused(): pl.pallas_call(functools.partial(fused_kernel, n, cols), out_shape=jax.Sh...  83.8 us

profile of v4, /device:TPU:0, one launch (start us, length us, event | category | flops | bytes accessed | tf_op | source)
XLA Modules:
  0.0 85.3 jit_solution(9004808511969084784)
XLA Ops:
  0.0 83.8 %shard_map.118 = bf16[8,5120]{1,0:T(8,128)(2,1)} custom-call(bf16[8,5120]{1,0:T(8,128)(2,1)} %hidden.1, bf16[2,8,5120]{2,1,0:T(8,128)(2,1)} %incoming.1, s32[1,16]{1,0:T(1,128)} %bitcast.15, bf16[3,96,5120]{2,1,0:T(8,128)(2,1)} %bitcast.12, bf16[320,5120]{1,0:T(8,128)(2,1)} %bitcast.8, bf16[320,5120]{1,0:T(8,128)(2,1)} %bitcast.9, ...), custom_call_target="tpu_custom_call" | custom-call | tf_op jit(solution)/shard_map/pallas_call | solution.py:928
  83.8 1.5 %copy.14 = bf16[8,5120]{1,0:T(8,128)(2,1)} copy(bf16[8,5120]{1,0:T(8,128)(2,1)} %shard_map.118) | data formatting | bytes 163840

commit v5 on v4

--- a/solution.py
+++ b/solution.py
@@ -395,17 +395,17 @@
                 turn_over_between(next(counts))
 
             line(1, every)
+            side(0, every)
+            line(2, every)
             chip(me)
-            side(0, every)
-            chip(along[1])
-            line(2, every)
-            chip(beside[0])
             side(1, every)
-            chip(along[2])
             line(3, every)
             late()
+            chip(along[1])
+            chip(beside[0])
+            chip(along[2])
+            side(2, every)
             chip(beside[1])
-            side(2, every)
             chip(along[3])
             side(3, every)
             chip(beside[2])

time: 85.5 us -> 84.1 us (0.984)
  Pallas kernels: 83.8 us -> 82.4 us
    pallas_call x1, Pallas kernels: 83.8 us -> 82.4 us  [per_device_fused(): pl.pallas_call(functools.partial(fused_kernel, n, cols), out_shape=jax.Sh...]
where the time goes in v5:
time: 84.1 us; the launch traced here: 83.9 us
  Pallas kernels  82.4 us (98%)
  local copies, waits for them, and re-layouts  1.53 us (2%)
    pallas_call x1, Pallas kernels, per_device_fused(): pl.pallas_call(functools.partial(fused_kernel, n, cols), out_shape=jax.Sh...  82.4 us

profile of v5, /device:TPU:0, one launch (start us, length us, event | category | flops | bytes accessed | tf_op | source)
XLA Modules:
  0.0 83.9 jit_solution(11164551490756259400)
XLA Ops:
  0.0 82.4 %shard_map.118 = bf16[8,5120]{1,0:T(8,128)(2,1)} custom-call(bf16[8,5120]{1,0:T(8,128)(2,1)} %hidden.1, bf16[2,8,5120]{2,1,0:T(8,128)(2,1)} %incoming.1, s32[1,16]{1,0:T(1,128)} %bitcast.15, bf16[3,96,5120]{2,1,0:T(8,128)(2,1)} %bitcast.12, bf16[320,5120]{1,0:T(8,128)(2,1)} %bitcast.8, bf16[320,5120]{1,0:T(8,128)(2,1)} %bitcast.9, ...), custom_call_target="tpu_custom_call" | custom-call | tf_op jit(solution)/shard_map/pallas_call | solution.py:928
  82.4 1.5 %copy.14 = bf16[8,5120]{1,0:T(8,128)(2,1)} copy(bf16[8,5120]{1,0:T(8,128)(2,1)} %shard_map.118) | data formatting | bytes 163840
